TPU v7x, 32 devices: a whole 2x2x4 slice. The times are simulated.
32 devices in a mesh: ctx: 8 (over y, x, core), ch: 4 (over z).
Axes of the slice: x: 2, y: 2, z: 4, core: 2. Of those that a mesh axis runs over, the one named last changes fastest.
Arguments:
- query_input: bfloat16 [1024, 4608], P('ctx', 'ch'), may hold values from -6 to 6
- key_input: bfloat16 [1024, 4608], P('ctx', 'ch'), may hold values from -6 to 6
- value_input: bfloat16 [1024, 4608], P('ctx', 'ch'), may hold values from -6 to 6
- filters: bfloat16 [4608, 128], P('ch'), may hold values from -1.7 to 1.7
- complement: int32 [4608], P('ch'), may hold values from 0 to 4607, as said below
- doc_lengths: int32 [16], replicated, may hold values from 1 to 256, 1024 in all
- cotangent: bfloat16 [1024, 4608], P('ctx', 'ch'), may hold values from -6 to 6
Outputs:
- mixer_out: bfloat16 [1024, 4608], P('ctx', 'ch')
- grad_query: bfloat16 [1024, 4608], P('ctx', 'ch')
- grad_key: bfloat16 [1024, 4608], P('ctx', 'ch')
- grad_value: bfloat16 [1024, 4608], P('ctx', 'ch')
- grad_filter: float32 [4608, 128], P('ch', 'ctx')
Inputs may be any that keep to these rules, and one draw needn't show every extreme that they name: complement pairs the channels: complement[complement[c]] = c and complement[c] != c for every channel c. `doc_lengths`: the 16 lengths sum to 1024.
All inputs are finite; a program needn't handle non-finite values.
Results may differ from a plain program's by a relative error of at most 0.0065.
Values may be sent and summed in bfloat16 or wider, within the bound.
A program may use at most 192 MiB of HBM per device.

v0:
```python
import jax
import jax.numpy as jnp
from jax import lax
from jax.sharding import PartitionSpec as P


def with_halo(shard, sides, width):
    for axis, dim in sides:
        size, length = (lax.axis_size(axis), shard.shape[dim])
        up = [(i, (i + 1) % size) for i in range(size - 1)]
        down = [(j, i) for i, j in up]
        last = lax.slice_in_dim(shard, length - width, length, axis=dim)
        first = lax.slice_in_dim(shard, 0, width, axis=dim)
        before = lax.ppermute(last, axis, up)
        after = lax.ppermute(first, axis, down)
        shard = jnp.concatenate([before, shard, after], axis=dim)
    return shard


def tap_masks(doc_lengths, places, taps_count):
    doc_ends = jnp.cumsum(doc_lengths)
    starts = doc_ends - doc_lengths
    inside = (places[:, None] >= starts[None, :]) & (places[:, None] < doc_ends[None, :])
    doc_first = jnp.sum(jnp.where(inside, starts[None, :], 0), axis=1)
    doc_last = jnp.sum(jnp.where(inside, doc_ends[None, :] - 1, 0), axis=1)
    offsets = jnp.arange(taps_count, dtype=jnp.int32)
    behind = places[:, None] - offsets[None, :] >= doc_first[:, None]
    forward = places[:, None] + offsets[None, :] <= doc_last[:, None]
    return (behind, forward)


def window_at(padded, first_row, row_count):
    return lax.slice_in_dim(padded, first_row, first_row + row_count, axis=0).astype(jnp.float32)


def forward_filters(filters, partner, padded_u, behind, forward, row_count):
    rim_width = filters.shape[1] - 1
    causal = jnp.zeros((row_count, filters.shape[0]), jnp.float32)
    anti = jnp.zeros((row_count, filters.shape[0]), jnp.float32)
    for offset in range(filters.shape[1]):
        earlier = window_at(padded_u, rim_width - offset, row_count)
        later = window_at(padded_u, rim_width + offset, row_count)
        causal = causal + jnp.where(
            behind[:, offset : offset + 1],
            filters[:, offset].astype(jnp.float32)[None, :] * earlier,
            0.0,
        )
        anti = anti + jnp.where(
            forward[:, offset : offset + 1],
            partner[:, offset].astype(jnp.float32)[None, :] * later,
            0.0,
        )
    return (causal, anti)


def backward_filters(filters, partner, padded_u, padded_r, upstream, behind, forward, row_count):
    rim_width = filters.shape[1] - 1
    upstream_f = upstream.astype(jnp.float32)
    ahead_sum = jnp.zeros((row_count, filters.shape[0]), jnp.float32)
    behind_sum = jnp.zeros((row_count, filters.shape[0]), jnp.float32)
    own_cols = []
    mirror_cols = []
    for offset in range(filters.shape[1]):
        low = rim_width - offset
        high = rim_width + offset
        before_mask = behind[:, offset : offset + 1]
        after_mask = forward[:, offset : offset + 1]
        later_r = window_at(padded_r, high, row_count)
        earlier_r = window_at(padded_r, low, row_count)
        earlier_u = window_at(padded_u, low, row_count)
        later_u = window_at(padded_u, high, row_count)
        ahead_sum = ahead_sum + jnp.where(
            after_mask, filters[:, offset].astype(jnp.float32)[None, :] * later_r, 0.0
        )
        behind_sum = behind_sum + jnp.where(
            before_mask, partner[:, offset].astype(jnp.float32)[None, :] * earlier_r, 0.0
        )
        own_cols.append(jnp.sum(jnp.where(before_mask, upstream_f * earlier_u, 0.0), axis=0))
        mirror_cols.append(jnp.sum(jnp.where(after_mask, upstream_f * later_u, 0.0), axis=0))
    return (ahead_sum, behind_sum, jnp.stack(own_cols, axis=1), jnp.stack(mirror_cols, axis=1))


def shards(query_input, key_input, value_input, filters, complement, doc_lengths, cotangent):
    row_count = query_input.shape[0]
    taps_count = filters.shape[1]
    rim_width = taps_count - 1
    device = lax.axis_index("ctx")
    places = device * row_count + jnp.arange(row_count, dtype=jnp.int32)
    behind, forward = tap_masks(doc_lengths, places, taps_count)

    def with_rims(field):
        return with_halo(field, (("ctx", 0),), rim_width)

    whole_filters = lax.all_gather(filters, "ch", axis=0, tiled=True)
    partner = jnp.take(whole_filters, complement, axis=0)
    key_f = key_input.astype(jnp.float32)
    value_f = value_input.astype(jnp.float32)
    query_f = query_input.astype(jnp.float32)
    cot_f = cotangent.astype(jnp.float32)
    product = (key_f * value_f).astype(jnp.bfloat16)
    upstream = (cot_f * query_f).astype(jnp.bfloat16)
    padded_u = with_rims(product)
    padded_r = None
    causal, anti = forward_filters(filters, partner, padded_u, behind, forward, row_count)
    strand_rc = anti.astype(jnp.bfloat16)
    combined = causal + strand_rc.astype(jnp.float32)
    mixer_out = (query_f * combined).astype(jnp.bfloat16)
    grad_query = (cot_f * combined).astype(jnp.bfloat16)
    padded_r = with_rims(upstream)
    ahead_sum, behind_sum, own_taps, mirrored_taps = backward_filters(
        filters, partner, padded_u, padded_r, upstream, behind, forward, row_count
    )
    rc_grad = behind_sum.astype(jnp.bfloat16)
    grad_product = ahead_sum + rc_grad.astype(jnp.float32)
    grad_key = (grad_product * value_f).astype(jnp.bfloat16)
    grad_value = (grad_product * key_f).astype(jnp.bfloat16)
    tied_own, tied_rc = (
        lax.psum_scatter(own_taps, "ctx", scatter_dimension=1, tiled=True),
        lax.psum_scatter(mirrored_taps, "ctx", scatter_dimension=1, tiled=True),
    )
    rc_all = lax.all_gather(tied_rc, "ch", axis=0, tiled=True)
    grad_filter = tied_own + jnp.take(rc_all, complement, axis=0)
    return (mixer_out, grad_query, grad_key, grad_value, grad_filter)


def solution(mesh):
    placed = (
        P("ctx", "ch"),
        P("ctx", "ch"),
        P("ctx", "ch"),
        P("ch", None),
        P("ch"),
        P(),
        P("ctx", "ch"),
    )
    return jax.shard_map(
        shards,
        mesh=mesh,
        in_specs=placed,
        out_specs=(P("ctx", "ch"), P("ctx", "ch"), P("ctx", "ch"), P("ctx", "ch"), P("ch", "ctx")),
        check_vma=False,
    )
```

profile of v0, /device:TPU:0, one launch (start us, length us, event | category | flops | bytes accessed | tf_op | source)
XLA Modules:
  0.0 1159.6 jit_solution(1995964167367138585)
XLA Ops:
  9.2 2.4 collective-permute-start
  23.2 3.0 convert_reduce_fusion.253
  26.3 3.8 convert_reduce_fusion.182
  30.1 3.8 convert_reduce_fusion.181
  33.8 4.0 convert_reduce_fusion.180
  37.8 3.2 convert_reduce_fusion.254
  41.2 3.8 convert_reduce_fusion.255
  45.6 3.8 convert_reduce_fusion.128
  49.8 24.4 %fusion.124 = f32[128,1152]{1,0:T(8,128)S(1)} fusion(bf16[128,1152]{1,0:T(8,128)(2,1)S(1)} %fusion.2, f32[1152]{0:T(1024)S(1)} %get-tuple-element.460, f32[1152]{0:T(1024)S(1)} %get-tuple-element.461, f32[1152]{0:T(1024)S(1)} %get-tuple-element.462, f32[1152]{0:T(1024)S(1)} %get-tuple-element.463, f32[1152]{0:T(1024)} %get-tuple-element.465, ...), kind=kLoop, calls=%fused_computation.1653 | loop fusion | flops 74760192 | bytes 1523072 | tf_op jit(solution)/shard_map/add | solution.py:43
  76.5 1.6 fusion.1402
  78.1 4.5 gather_fusion
  83.5 2.4 convert_reduce_fusion.122
  86.1 3.8 convert_reduce_fusion.54
  89.9 3.2 convert_reduce_fusion.123
  93.2 4.0 convert_reduce_fusion.124
  97.2 3.8 convert_reduce_fusion.125
  101.0 3.8 convert_reduce_fusion.126
  104.8 3.8 convert_reduce_fusion.127
  109.3 24.9 %fusion.379 = f32[128,1152]{1,0:T(8,128)S(1)} fusion(bf16[128,1152]{1,0:T(8,128)(2,1)S(1)} %fusion.2, f32[1152]{0:T(1024)} %get-tuple-element.337, f32[1152]{0:T(1024)} %get-tuple-element.338, f32[1152]{0:T(1024)} %get-tuple-element.339, f32[1152]{0:T(1024)} %get-tuple-element.340, f32[1152]{0:T(1024)} %get-tuple-element.341, f32[1152]{0:T(1024)} %get-tuple-element.342, ...), kind=kLoop, calls=%fused_computation.1908 | loop fusion | flops 74760192 | bytes 1523072 | tf_op jit(solution)/shard_map/add | solution.py:48
  134.6 234.6 %fusion.514 = (bf16[128,1152]{1,0:T(8,128)(2,1)}, f32[128,1152]{1,0:T(8,128)S(1)}) fusion(bf16[128,1152]{1,0:T(8,128)(2,1)S(1)} %copy-done.13, bf16[127,1152]{1,0:T(8,128)(2,1)S(1)} %collective-permute-done.1, bf16[128,1152]{1,0:T(8,128)(2,1)S(1)} %fusion.2, f32[1152]{0:T(1024)} %get-tuple-element.280, pred[128]{0:T(512)(128)(4,1)} %get-tuple-element.870, ...), kind=kLoop, calls=%fused_computation.2043 | loop fusion | flops 105578496 | bytes 9658624 | tf_op jit(solution)/shard_map/convert_element_type | solution.py:108
  369.2 1.5 fusion.1033
  370.9 1.5 fusion.807
  372.5 1.6 fusion.809
  374.2 1.5 fusion.811
  375.9 1.6 fusion.813
  377.6 1.5 fusion.815
  379.2 1.5 fusion.817
  380.9 1.5 fusion.819
  384.2 2.2 fusion.781
  386.6 2.2 fusion.783
  389.0 3.0 fusion.785
  395.1 1.5 fusion.793
  396.8 1.5 fusion.795
  398.4 1.6 fusion.797
  400.1 1.5 fusion.799
  402.4 1.5 fusion.801
  409.4 1.6 fusion.1039
  429.6 1.5 fusion.1053
  444.3 1.5 fusion.1059
  454.4 2.3 fusion.1063
  460.3 1.9 fusion.1065
  465.8 2.4 fusion.1067
  471.8 1.9 fusion.1069
  477.2 1.6 fusion.803
  482.4 5.1 collective-permute-start.3
  493.9 13.7 %stack.902 = f32[1152,128]{0,1:T(8,128)} concatenate(f32[1152,1]{0,1:T(1,128)S(1)} %stack.774, f32[1152,1]{0,1:T(1,128)S(1)} %stack.775, f32[1152,1]{0,1:T(1,128)S(1)} %stack.776, f32[1152,1]{0,1:T(1,128)S(1)} %stack.777, f32[1152,1]{0,1:T(1,128)S(1)} %stack.778, f32[1152,1]{0,1:T(1,128)S(1)} %stack.779, f32[1152,1]{0,1:T(1,128)S(1)} %stack.780, f32[1152,1]{0,1:T(1,128)S(1)} %stack.781, ...), dimensions={1} | concatenate | bytes 1179648 | tf_op jit(solution)/shard_map/stack | solution.py:80
  507.7 2.6 fusion.1071
  510.4 1.6 fusion.1075
  512.0 2.9 fusion.1073
  517.0 14.6 %stack.1031 = f32[1152,128]{0,1:T(8,128)} concatenate(f32[1152,1]{0,1:T(1,128)S(1)} %stack.903, f32[1152,1]{0,1:T(1,128)S(1)} %stack.904, f32[1152,1]{0,1:T(1,128)S(1)} %stack.905, f32[1152,1]{0,1:T(1,128)S(1)} %stack.906, f32[1152,1]{0,1:T(1,128)S(1)} %stack.907, f32[1152,1]{0,1:T(1,128)S(1)} %stack.908, f32[1152,1]{0,1:T(1,128)S(1)} %stack.909, f32[1152,1]{0,1:T(1,128)S(1)} %stack.910, ...), dimensions={1} | concatenate | bytes 1179648 | tf_op jit(solution)/shard_map/stack | solution.py:80
  533.0 1.6 fusion.1165
  534.6 1.6 fusion.1183
  536.2 1.6 fusion.1174
  537.9 1.6 fusion.1147
  539.4 1.6 fusion.1129
  541.1 1.7 fusion.1138
  542.7 1.6 fusion.1156
  544.4 1.7 fusion.1120
  551.9 1.6 fusion.1250
  553.8 1.6 fusion.1251
  555.8 266.9 %add_convert_fusion = bf16[128,1152]{1,0:T(8,128)(2,1)} fusion(bf16[128,1152]{1,0:T(8,128)(2,1)} %get-tuple-element.733, bf16[128,1152]{1,0:T(8,128)(2,1)} %get-tuple-element.732, bf16[128,1152]{1,0:T(8,128)(2,1)} %get-tuple-element.734, bf16[128,1152]{1,0:T(8,128)(2,1)} %get-tuple-element.707, bf16[128,1152]{1,0:T(8,128)(2,1)} %get-tuple-element.706, ...), kind=kLoop, calls=%fused_computation.2865 | loop fusion | flops 93634560 | bytes 26846336 | tf_op jit(solution)/shard_map/convert_element_type | solution.py:113
  822.8 279.3 %fusion.1 = (bf16[128,1152]{1,0:T(8,128)(2,1)}, f32[128,1152]{1,0:T(8,128)S(1)}) fusion(bf16[128,1152]{1,0:T(8,128)(2,1)} %param.8, bf16[128,1152]{1,0:T(8,128)(2,1)} %add_convert_fusion, bf16[128,1152]{1,0:T(8,128)(2,1)} %get-tuple-element.625, f32[1152]{0:T(1024)} %get-tuple-element.464, pred[128]{0:T(512)(128)(4,1)} %get-tuple-element.870, ...), kind=kLoop, calls=%fused_computation.1530 | loop fusion | flops 95109120 | bytes 27440896 | tf_op jit(solution)/shard_map/convert_element_type | solution.py:116
  1105.1 42.3 %all_gather.7 = f32[4608,16]{1,0:T(8,128)S(1)} all-gather(f32[1152,16]{1,0:T(8,128)S(1)} %copy.283), channel_id=1, replica_groups=mesh['ctx'=8,'ch'=4] {'ch'}, dimensions={0}, use_global_device_ids=true | all-gather | bytes 368640 | tf_op jit(solution)/shard_map/all_gather | solution.py:121
  1147.4 3.1 gather_fusion.1
  (1034 shorter events, 106.3 us)
Async XLA Ops:
  7.2 70.9 %all-gather.2.cloned.1.call-start = ((), (), s32[]{:S(2)}) async-start(), calls=%async_computation.2 | async-start | bytes 1474560 | tf_op jit(solution)/shard_map/all_gather | solution.py:94
  7.9 1094.9 %reduce-scatter.7.cloned.1.call-start = ((), (), s32[]{:S(2)}) async-start(), calls=%async_computation.3 | async-start | bytes 663552
  9.2 40.2 %collective-permute-start = (bf16[127,1152]{1,0:T(8,128)(2,1)S(1)}, bf16[127,1152]{1,0:T(8,128)(2,1)S(1)}, u32[]{:S(2)}, u32[]{:S(2)}) collective-permute-start(bf16[127,1152]{1,0:T(8,128)(2,1)S(1)} %get-tuple-element.739), channel_id=1, source_target_pairs={{0,4},{4,8},{8,12},{12,16},{16,20},{20,24},{24,28},{1,5},{5,9},{9,... | collective-permute-start | bytes 877832 | tf_op jit(solution)/shard_map/ppermute | solution.py:14
  11.6 62.6 %collective-permute-start.1 = (bf16[127,1152]{1,0:T(8,128)(2,1)S(1)}, bf16[127,1152]{1,0:T(8,128)(2,1)S(1)}, u32[]{:S(2)}, u32[]{:S(2)}) collective-permute-start(bf16[127,1152]{1,0:T(8,128)(2,1)S(1)} %get-tuple-element.740), channel_id=1, source_target_pairs={{4,0},{8,4},{12,8},{16,12},{20,16},{24,20},{28,24},{5,1},{9,5},{13... | collective-permute-start | bytes 877832 | tf_op jit(solution)/shard_map/ppermute | solution.py:15
  104.7 29.5 %copy-start.9 = (bf16[128,1152]{1,0:T(8,128)(2,1)S(1)}, bf16[128,1152]{1,0:T(8,128)(2,1)}, u32[]{:S(2)}) copy-start(bf16[128,1152]{1,0:T(8,128)(2,1)} %get-tuple-element.725) | copy-start | bytes 884740
  104.7 29.5 %copy-start.10 = (bf16[128,1152]{1,0:T(8,128)(2,1)S(1)}, bf16[128,1152]{1,0:T(8,128)(2,1)}, u32[]{:S(2)}) copy-start(bf16[128,1152]{1,0:T(8,128)(2,1)} %get-tuple-element.726) | copy-start | bytes 884740
  104.8 29.5 %copy-start.11 = (bf16[128,1152]{1,0:T(8,128)(2,1)S(1)}, bf16[128,1152]{1,0:T(8,128)(2,1)}, u32[]{:S(2)}) copy-start(bf16[128,1152]{1,0:T(8,128)(2,1)} %get-tuple-element.727) | copy-start | bytes 884740
  104.8 29.5 %copy-start.12 = (bf16[128,1152]{1,0:T(8,128)(2,1)S(1)}, bf16[128,1152]{1,0:T(8,128)(2,1)}, u32[]{:S(2)}) copy-start(bf16[128,1152]{1,0:T(8,128)(2,1)} %get-tuple-element.728) | copy-start | bytes 884740
  104.8 29.5 %copy-start.13 = (bf16[128,1152]{1,0:T(8,128)(2,1)S(1)}, bf16[128,1152]{1,0:T(8,128)(2,1)}, u32[]{:S(2)}) copy-start(bf16[128,1152]{1,0:T(8,128)(2,1)} %param.13) | copy-start | bytes 884740
  104.8 29.5 %copy-start.14 = (bf16[128,1152]{1,0:T(8,128)(2,1)S(1)}, bf16[128,1152]{1,0:T(8,128)(2,1)}, u32[]{:S(2)}) copy-start(bf16[128,1152]{1,0:T(8,128)(2,1)} %get-tuple-element.729) | copy-start | bytes 884740
  104.8 29.5 %copy-start.15 = (bf16[128,1152]{1,0:T(8,128)(2,1)S(1)}, bf16[128,1152]{1,0:T(8,128)(2,1)}, u32[]{:S(2)}) copy-start(bf16[128,1152]{1,0:T(8,128)(2,1)} %get-tuple-element.730) | copy-start | bytes 884740
  108.6 25.7 %copy-start.2 = (bf16[128,1152]{1,0:T(8,128)(2,1)S(1)}, bf16[128,1152]{1,0:T(8,128)(2,1)}, u32[]{:S(2)}) copy-start(bf16[128,1152]{1,0:T(8,128)(2,1)} %get-tuple-element.718) | copy-start | bytes 884740
  108.6 25.7 %copy-start.3 = (bf16[128,1152]{1,0:T(8,128)(2,1)S(1)}, bf16[128,1152]{1,0:T(8,128)(2,1)}, u32[]{:S(2)}) copy-start(bf16[128,1152]{1,0:T(8,128)(2,1)} %get-tuple-element.719) | copy-start | bytes 884740
  108.6 25.7 %copy-start.4 = (bf16[128,1152]{1,0:T(8,128)(2,1)S(1)}, bf16[128,1152]{1,0:T(8,128)(2,1)}, u32[]{:S(2)}) copy-start(bf16[128,1152]{1,0:T(8,128)(2,1)} %get-tuple-element.720) | copy-start | bytes 884740
  108.6 25.7 %copy-start.5 = (bf16[128,1152]{1,0:T(8,128)(2,1)S(1)}, bf16[128,1152]{1,0:T(8,128)(2,1)}, u32[]{:S(2)}) copy-start(bf16[128,1152]{1,0:T(8,128)(2,1)} %get-tuple-element.721) | copy-start | bytes 884740
  108.6 25.7 %copy-start.6 = (bf16[128,1152]{1,0:T(8,128)(2,1)S(1)}, bf16[128,1152]{1,0:T(8,128)(2,1)}, u32[]{:S(2)}) copy-start(bf16[128,1152]{1,0:T(8,128)(2,1)} %get-tuple-element.722) | copy-start | bytes 884740
  108.7 25.7 %copy-start.7 = (bf16[128,1152]{1,0:T(8,128)(2,1)S(1)}, bf16[128,1152]{1,0:T(8,128)(2,1)}, u32[]{:S(2)}) copy-start(bf16[128,1152]{1,0:T(8,128)(2,1)} %get-tuple-element.723) | copy-start | bytes 884740
  108.7 25.7 %copy-start.8 = (bf16[128,1152]{1,0:T(8,128)(2,1)S(1)}, bf16[128,1152]{1,0:T(8,128)(2,1)}, u32[]{:S(2)}) copy-start(bf16[128,1152]{1,0:T(8,128)(2,1)} %get-tuple-element.724) | copy-start | bytes 884740
  108.7 25.7 %copy-start.136 = (f32[1152]{0:T(1024)S(1)}, f32[1152]{0:T(1024)}, u32[]{:S(2)}) copy-start(f32[1152]{0:T(1024)} %get-tuple-element.738) | copy-start | bytes 13828
  108.7 25.7 %copy-start.137 = (f32[1152]{0:T(1024)S(1)}, f32[1152]{0:T(1024)}, u32[]{:S(2)}) copy-start(f32[1152]{0:T(1024)} %get-tuple-element.407) | copy-start | bytes 13828
  108.7 25.7 %copy-start.138 = (f32[1152]{0:T(1024)S(1)}, f32[1152]{0:T(1024)}, u32[]{:S(2)}) copy-start(f32[1152]{0:T(1024)} %get-tuple-element.408) | copy-start | bytes 13828
  108.7 25.7 %copy-start.139 = (f32[1152]{0:T(1024)S(1)}, f32[1152]{0:T(1024)}, u32[]{:S(2)}) copy-start(f32[1152]{0:T(1024)} %get-tuple-element.409) | copy-start | bytes 13828
  108.7 25.7 %copy-start.140 = (f32[1152]{0:T(1024)S(1)}, f32[1152]{0:T(1024)}, u32[]{:S(2)}) copy-start(f32[1152]{0:T(1024)} %get-tuple-element.410) | copy-start | bytes 13828
  108.7 25.7 %copy-start.141 = (f32[1152]{0:T(1024)S(1)}, f32[1152]{0:T(1024)}, u32[]{:S(2)}) copy-start(f32[1152]{0:T(1024)} %get-tuple-element.411) | copy-start | bytes 13828
  108.7 25.7 %copy-start.142 = (f32[1152]{0:T(1024)S(1)}, f32[1152]{0:T(1024)}, u32[]{:S(2)}) copy-start(f32[1152]{0:T(1024)} %get-tuple-element.412) | copy-start | bytes 13828
  108.7 25.7 %copy-start.143 = (f32[1152]{0:T(1024)S(1)}, f32[1152]{0:T(1024)}, u32[]{:S(2)}) copy-start(f32[1152]{0:T(1024)} %get-tuple-element.413) | copy-start | bytes 13828
  108.8 25.7 %copy-start.144 = (f32[1152]{0:T(1024)S(1)}, f32[1152]{0:T(1024)}, u32[]{:S(2)}) copy-start(f32[1152]{0:T(1024)} %get-tuple-element.414) | copy-start | bytes 13828
  108.8 25.7 %copy-start.145 = (f32[1152]{0:T(1024)S(1)}, f32[1152]{0:T(1024)}, u32[]{:S(2)}) copy-start(f32[1152]{0:T(1024)} %get-tuple-element.415) | copy-start | bytes 13828
  108.8 25.7 %copy-start.146 = (f32[1152]{0:T(1024)S(1)}, f32[1152]{0:T(1024)}, u32[]{:S(2)}) copy-start(f32[1152]{0:T(1024)} %get-tuple-element.416) | copy-start | bytes 13828
  108.8 25.7 %copy-start.147 = (f32[1152]{0:T(1024)S(1)}, f32[1152]{0:T(1024)}, u32[]{:S(2)}) copy-start(f32[1152]{0:T(1024)} %get-tuple-element.417) | copy-start | bytes 13828
  108.8 25.7 %copy-start.148 = (f32[1152]{0:T(1024)S(1)}, f32[1152]{0:T(1024)}, u32[]{:S(2)}) copy-start(f32[1152]{0:T(1024)} %get-tuple-element.418) | copy-start | bytes 13828
  108.8 25.7 %copy-start.149 = (f32[1152]{0:T(1024)S(1)}, f32[1152]{0:T(1024)}, u32[]{:S(2)}) copy-start(f32[1152]{0:T(1024)} %get-tuple-element.419) | copy-start | bytes 13828
  108.8 25.7 %copy-start.150 = (f32[1152]{0:T(1024)S(1)}, f32[1152]{0:T(1024)}, u32[]{:S(2)}) copy-start(f32[1152]{0:T(1024)} %get-tuple-element.420) | copy-start | bytes 13828
  108.8 25.7 %copy-start.151 = (f32[1152]{0:T(1024)S(1)}, f32[1152]{0:T(1024)}, u32[]{:S(2)}) copy-start(f32[1152]{0:T(1024)} %get-tuple-element.421) | copy-start | bytes 13828
  108.8 25.7 %copy-start.152 = (f32[1152]{0:T(1024)S(1)}, f32[1152]{0:T(1024)}, u32[]{:S(2)}) copy-start(f32[1152]{0:T(1024)} %get-tuple-element.422) | copy-start | bytes 13828
  108.8 25.7 %copy-start.153 = (f32[1152]{0:T(1024)S(1)}, f32[1152]{0:T(1024)}, u32[]{:S(2)}) copy-start(f32[1152]{0:T(1024)} %get-tuple-element.423) | copy-start | bytes 13828
  108.9 25.7 %copy-start.154 = (f32[1152]{0:T(1024)S(1)}, f32[1152]{0:T(1024)}, u32[]{:S(2)}) copy-start(f32[1152]{0:T(1024)} %get-tuple-element.424) | copy-start | bytes 13828
  108.9 25.7 %copy-start.155 = (f32[1152]{0:T(1024)S(1)}, f32[1152]{0:T(1024)}, u32[]{:S(2)}) copy-start(f32[1152]{0:T(1024)} %get-tuple-element.425) | copy-start | bytes 13828
  108.9 25.7 %copy-start.156 = (f32[1152]{0:T(1024)S(1)}, f32[1152]{0:T(1024)}, u32[]{:S(2)}) copy-start(f32[1152]{0:T(1024)} %get-tuple-element.426) | copy-start | bytes 13828
  108.9 25.7 %copy-start.157 = (f32[1152]{0:T(1024)S(1)}, f32[1152]{0:T(1024)}, u32[]{:S(2)}) copy-start(f32[1152]{0:T(1024)} %get-tuple-element.427) | copy-start | bytes 13828
  108.9 25.7 %copy-start.158 = (f32[1152]{0:T(1024)S(1)}, f32[1152]{0:T(1024)}, u32[]{:S(2)}) copy-start(f32[1152]{0:T(1024)} %get-tuple-element.428) | copy-start | bytes 13828
  108.9 25.7 %copy-start.159 = (f32[1152]{0:T(1024)S(1)}, f32[1152]{0:T(1024)}, u32[]{:S(2)}) copy-start(f32[1152]{0:T(1024)} %get-tuple-element.429) | copy-start | bytes 13828
  134.6 234.6 %copy-start.17 = (bf16[128,1152]{1,0:T(8,128)(2,1)S(1)}, bf16[128,1152]{1,0:T(8,128)(2,1)}, u32[]{:S(2)}) copy-start(bf16[128,1152]{1,0:T(8,128)(2,1)} %param.7) | copy-start | bytes 884740
  439.8 25.9 %copy-start.258 = (pred[128]{0:T(512)(128)(4,1)S(1)}, pred[128]{0:T(512)(128)(4,1)}, u32[]{:S(2)}) copy-start(pred[128]{0:T(512)(128)(4,1)} %get-tuple-element.874) | copy-start | bytes 388
  439.8 25.9 %copy-start.320 = (pred[128]{0:T(512)(128)(4,1)S(1)}, pred[128]{0:T(512)(128)(4,1)}, u32[]{:S(2)}) copy-start(pred[128]{0:T(512)(128)(4,1)} %get-tuple-element.976) | copy-start | bytes 388
  439.8 25.9 %copy-start.321 = (pred[128]{0:T(512)(128)(4,1)S(1)}, pred[128]{0:T(512)(128)(4,1)}, u32[]{:S(2)}) copy-start(pred[128]{0:T(512)(128)(4,1)} %get-tuple-element.977) | copy-start | bytes 388
  439.8 25.9 %copy-start.322 = (pred[128]{0:T(512)(128)(4,1)S(1)}, pred[128]{0:T(512)(128)(4,1)}, u32[]{:S(2)}) copy-start(pred[128]{0:T(512)(128)(4,1)} %get-tuple-element.978) | copy-start | bytes 388
  439.8 25.9 %copy-start.323 = (pred[128]{0:T(512)(128)(4,1)S(1)}, pred[128]{0:T(512)(128)(4,1)}, u32[]{:S(2)}) copy-start(pred[128]{0:T(512)(128)(4,1)} %get-tuple-element.979) | copy-start | bytes 388
  439.9 25.9 %copy-start.324 = (pred[128]{0:T(512)(128)(4,1)S(1)}, pred[128]{0:T(512)(128)(4,1)}, u32[]{:S(2)}) copy-start(pred[128]{0:T(512)(128)(4,1)} %get-tuple-element.980) | copy-start | bytes 388
  444.2 27.5 %copy-start.257 = (pred[128]{0:T(512)(128)(4,1)S(1)}, pred[128]{0:T(512)(128)(4,1)}, u32[]{:S(2)}) copy-start(pred[128]{0:T(512)(128)(4,1)} %get-tuple-element.873) | copy-start | bytes 388
  444.2 27.5 %copy-start.306 = (pred[128]{0:T(512)(128)(4,1)S(1)}, pred[128]{0:T(512)(128)(4,1)}, u32[]{:S(2)}) copy-start(pred[128]{0:T(512)(128)(4,1)} %get-tuple-element.984) | copy-start | bytes 388
  444.2 27.5 %copy-start.307 = (pred[128]{0:T(512)(128)(4,1)S(1)}, pred[128]{0:T(512)(128)(4,1)}, u32[]{:S(2)}) copy-start(pred[128]{0:T(512)(128)(4,1)} %get-tuple-element.985) | copy-start | bytes 388
  444.3 27.5 %copy-start.308 = (pred[128]{0:T(512)(128)(4,1)S(1)}, pred[128]{0:T(512)(128)(4,1)}, u32[]{:S(2)}) copy-start(pred[128]{0:T(512)(128)(4,1)} %get-tuple-element.986) | copy-start | bytes 388
  444.3 27.5 %copy-start.325 = (pred[128]{0:T(512)(128)(4,1)S(1)}, pred[128]{0:T(512)(128)(4,1)}, u32[]{:S(2)}) copy-start(pred[128]{0:T(512)(128)(4,1)} %get-tuple-element.981) | copy-start | bytes 388
  444.3 27.5 %copy-start.326 = (pred[128]{0:T(512)(128)(4,1)S(1)}, pred[128]{0:T(512)(128)(4,1)}, u32[]{:S(2)}) copy-start(pred[128]{0:T(512)(128)(4,1)} %get-tuple-element.982) | copy-start | bytes 388
  449.4 27.8 %copy-start.213 = (pred[128]{0:T(512)(128)(4,1)S(1)}, pred[128]{0:T(512)(128)(4,1)}, u32[]{:S(2)}) copy-start(pred[128]{0:T(512)(128)(4,1)} %get-tuple-element.751) | copy-start | bytes 388
  454.4 33.1 %copy-start.212 = (pred[128]{0:T(512)(128)(4,1)S(1)}, pred[128]{0:T(512)(128)(4,1)}, u32[]{:S(2)}) copy-start(pred[128]{0:T(512)(128)(4,1)} %get-tuple-element.750) | copy-start | bytes 388
  460.3 32.2 %copy-start.243 = (pred[128]{0:T(512)(128)(4,1)S(1)}, pred[128]{0:T(512)(128)(4,1)}, u32[]{:S(2)}) copy-start(pred[128]{0:T(512)(128)(4,1)} %get-tuple-element.764) | copy-start | bytes 388
  460.3 32.2 %copy-start.349 = (pred[128]{0:T(512)(128)(4,1)S(1)}, pred[128]{0:T(512)(128)(4,1)}, u32[]{:S(2)}) copy-start(pred[128]{0:T(512)(128)(4,1)} %get-tuple-element.888) | copy-start | bytes 388
  482.4 10.1 collective-permute-start.3
  507.7 596.3 %reduce-scatter.9.cloned.1.call-start = ((), (), s32[]{:S(2)}) async-start(), calls=%async_computation.4 | async-start | bytes 663552
  515.1 31.0 %collective-permute-start.2 = (bf16[127,1152]{1,0:T(8,128)(2,1)S(1)}, bf16[127,1152]{1,0:T(8,128)(2,1)S(1)}, u32[]{:S(2)}, u32[]{:S(2)}) collective-permute-start(bf16[127,1152]{1,0:T(8,128)(2,1)S(1)} %get-tuple-element.735), channel_id=1, source_target_pairs={{4,0},{8,4},{12,8},{16,12},{20,16},{24,20},{28,24},{5,1},{9,5},{13... | collective-permute-start | bytes 877832 | tf_op jit(solution)/shard_map/ppermute | solution.py:15
  822.8 279.3 %copy-start.16 = (bf16[128,1152]{1,0:T(8,128)(2,1)S(1)}, bf16[128,1152]{1,0:T(8,128)(2,1)}, u32[]{:S(2)}) copy-start(bf16[128,1152]{1,0:T(8,128)(2,1)} %param.9) | copy-start | bytes 884740
  1102.8 44.5 %copy-start.135 = (s32[2048]{0:T(1024)S(1)}, s32[2048]{0:T(1024)}, u32[]{:S(2)}) copy-start(s32[2048]{0:T(1024)} %pad_clamp_fusion) | copy-start | bytes 24580
  (294 other events, 3675.9 us)
Sparse Core Ops, SparseCore 0:
  9.6 32.9 all-gather.1
  507.8 37.6 reduce-scatter.6
  548.7 34.3 reduce-scatter.8
where the time goes:
time: 1170 us; the launch traced here: 1160 us
  other arithmetic  979 us (84%)
  local copies, waits for them, and re-layouts  107 us (9%)
  blocking collectives  42.3 us (4%)
  between operations  20.7 us (2%)
    convert_element_type x1, other arithmetic, shards(): grad_value = (grad_product * key_f).astype(jnp.bfloat16)  279 us
    convert_element_type x1, other arithmetic, shards(): rc_grad = behind_sum.astype(jnp.bfloat16)  267 us
    convert_element_type x1, other arithmetic, shards(): grad_query = (cot_f * combined).astype(jnp.bfloat16)  235 us
    another operation x129, local copies, waits for them, and re-layouts, backward_filters(): jnp.stack(mirror_cols, axis=1)  59.3 us
    all_gather x1, blocking collectives, shards(): rc_all = lax.all_gather(tied_rc, 'ch', axis=0, tiled=True)  42.3 us
    reduce_sum x23, other arithmetic, backward_filters(): jnp.sum(jnp.where(after_mask, upstream_f * later_u, 0.0), axis=0)  33.3 us
    reduce_sum x21, other arithmetic, backward_filters(): jnp.sum(jnp.where(before_mask, upstream_f * earlier_u, 0.0), axis=0)  32.8 us
    concatenate x22, other arithmetic, with_halo(): shard = jnp.concatenate([before, shard, after], axis=dim)  27.4 us
  transfers between devices with their start and end apart: 7, of which 0 were waited for; matrix products, arithmetic and copies ran while one was open for 57% of the time, Pallas kernels for 0%

commit v1 on v0

v1 whole, which is shorter than its diff:
```python
import functools

import jax
import jax.numpy as jnp
import numpy as np
from jax import lax
from jax.experimental import pallas as pl
from jax.experimental.pallas import tpu as pltpu
from jax.sharding import PartitionSpec as P

F32, BF16 = jnp.float32, jnp.bfloat16


def split_bf16(table):
    high = table.astype(BF16)
    low = (table - high.astype(np.float64)).astype(BF16)
    return high, low


def fourier_tables(rows, taps, owners):
    length = 3 * rows
    angle = 2.0 * np.pi * (np.arange(length // 2) + 0.5) / length
    places = np.arange(length) - rows
    turns = angle[:, None] * places[None, :]
    analyse = np.concatenate([np.cos(turns), -np.sin(turns)], axis=0)
    own = np.arange(rows)[:, None] * angle[None, :]
    rebuild = np.concatenate([np.cos(own), -np.sin(own)], axis=1) * (2.0 / length)
    lags = angle[:, None] * np.arange(taps)[None, :]
    causal = np.concatenate([np.cos(lags), -np.sin(lags)], axis=0)
    anti = np.concatenate([np.cos(lags), np.sin(lags)], axis=0)
    share = taps // owners
    offsets = np.concatenate([
        np.concatenate([np.arange(t * share, (t + 1) * share), -np.arange(t * share, (t + 1) * share)])
        for t in range(owners)
    ])
    spread = offsets[:, None] * angle[None, :]
    tap_rows = np.concatenate([np.cos(spread), -np.sin(spread)], axis=1) * (2.0 / length)
    return (
        analyse.astype(BF16),
        rebuild.astype(BF16),
        *split_bf16(causal),
        *split_bf16(anti),
        *split_bf16(tap_rows),
    )


def mm(a, b):
    return jnp.dot(a, b, preferred_element_type=F32)


def mm_t(a, b):
    return lax.dot_general(a, b, (((1,), (1,)), ((), ())), preferred_element_type=F32)


def mix_kernel(
    lens, query, key, value, cot, u_prev, u_next, r_prev, r_next, taps_own, taps_partner,
    analyse, rebuild, causal_hi, causal_lo, anti_hi, anti_lo, tap_hi, tap_lo,
    mixer_out, grad_query, grad_key, grad_value, tap_sums,
    spectrum, window_u, own_r, acc_y, acc_p, acc_g, z_ref, q_ref,
):
    rows = query.shape[0]
    half = analyse.shape[0] // 2
    first_place = lax.axis_index("ctx") * rows

    f, g = taps_own[...], taps_partner[...]
    spectrum[...] = (
        mm_t(causal_hi[...], f) + mm_t(causal_lo[...], f) + mm_t(anti_hi[...], g) + mm_t(anti_lo[...], g)
    )
    window_u[0:rows] = u_prev[...]
    window_u[rows : 2 * rows] = (key[...].astype(F32) * value[...].astype(F32)).astype(BF16)
    window_u[2 * rows : 3 * rows] = u_next[...]
    own_r[...] = (cot[...].astype(F32) * query[...].astype(F32)).astype(BF16)
    acc_y[...] = jnp.zeros_like(acc_y)
    acc_p[...] = jnp.zeros_like(acc_p)
    acc_g[...] = jnp.zeros_like(acc_g)

    def document(d, start):
        end = start + lens[d]

        @pl.when((start < first_place + rows) & (end > first_place))
        def _():
            low, high = start - first_place, end - first_place
            lane = lax.broadcasted_iota(jnp.int32, (1, 3 * rows), 1) - rows
            here = ((lane >= low) & (lane < high)).astype(F32).astype(BF16)
            masked = analyse[...] * here
            column = lax.broadcasted_iota(jnp.int32, (rows, 1), 0)
            kept = ((column >= low) & (column < high)).astype(F32).astype(BF16)
            back = rebuild[...] * kept
            u_hat = mm(masked, window_u[...])
            o_hat = mm(masked[:, rows : 2 * rows], own_r[...])
            r_hat = o_hat + mm(masked[:, :rows], r_prev[...]) + mm(masked[:, 2 * rows :], r_next[...])
            h_re, h_im = spectrum[:half], spectrum[half:]
            u_re, u_im = u_hat[:half], u_hat[half:]
            r_re, r_im = r_hat[:half], r_hat[half:]
            o_re, o_im = o_hat[:half], o_hat[half:]
            z_ref[:half] = (h_re * u_re - h_im * u_im).astype(BF16)
            z_ref[half:] = (h_re * u_im + h_im * u_re).astype(BF16)
            q_ref[:half] = (h_re * r_re + h_im * r_im).astype(BF16)
            q_ref[half:] = (h_re * r_im - h_im * r_re).astype(BF16)
            acc_g[:half] += o_re * u_re + o_im * u_im
            acc_g[half:] += o_im * u_re - o_re * u_im
            acc_y[...] += mm(back, z_ref[...])
            acc_p[...] += mm(back, q_ref[...])

        return end

    lax.fori_loop(0, lens.shape[0], document, jnp.int32(0))
    combined, grad_product = acc_y[...], acc_p[...]
    mixer_out[...] = (query[...].astype(F32) * combined).astype(BF16)
    grad_query[...] = (cot[...].astype(F32) * combined).astype(BF16)
    grad_key[...] = (grad_product * value[...].astype(F32)).astype(BF16)
    grad_value[...] = (grad_product * key[...].astype(F32)).astype(BF16)
    g_sum = acc_g[...]
    g_hi = g_sum.astype(BF16)
    g_lo = (g_sum - g_hi.astype(F32)).astype(BF16)
    tap_sums[...] = mm(tap_hi[...], g_hi) + mm(tap_hi[...], g_lo) + mm(tap_lo[...], g_hi)


def channel_block(channels):
    for block in (384, 256, 128):
        if channels % block == 0:
            return block
    return channels


def mix(doc_lengths, fields, filters, partner, owners):
    rows, channels = fields[0].shape
    taps = filters.shape[1]
    block = channel_block(channels)
    tables = fourier_tables(rows, taps, owners)
    length = 3 * rows
    field_spec = pl.BlockSpec((rows, block), lambda i: (0, i))
    filter_spec = pl.BlockSpec((block, taps), lambda i: (i, 0))
    table_specs = [pl.BlockSpec(t.shape, lambda i: (0, 0)) for t in tables]
    return pl.pallas_call(
        mix_kernel,
        grid=(channels // block,),
        in_specs=[pl.BlockSpec(memory_space=pltpu.SMEM)]
        + [field_spec] * 8
        + [filter_spec] * 2
        + table_specs,
        out_specs=[field_spec] * 4 + [pl.BlockSpec((2 * taps, block), lambda i: (0, i))],
        out_shape=[jax.ShapeDtypeStruct((rows, channels), BF16)] * 4
        + [jax.ShapeDtypeStruct((2 * taps, channels), F32)],
        scratch_shapes=[
            pltpu.VMEM((length, block), F32),
            pltpu.VMEM((length, block), BF16),
            pltpu.VMEM((rows, block), BF16),
            pltpu.VMEM((rows, block), F32),
            pltpu.VMEM((rows, block), F32),
            pltpu.VMEM((length, block), F32),
            pltpu.VMEM((length, block), BF16),
            pltpu.VMEM((length, block), BF16),
        ],
        name="mix",
    )(doc_lengths, *fields, filters, partner, *[jnp.asarray(t) for t in tables])


def gather_relative(shard, axis):
    size = lax.axis_size(axis)
    blocks = [shard]
    for step in range(1, size):
        blocks.append(lax.ppermute(shard, axis, [(i, (i + step) % size) for i in range(size)]))
    return jnp.concatenate(blocks, axis=0)


def reduce_owned(pieces, axis):
    size = lax.axis_size(axis)
    me = lax.axis_index(axis)
    if size > 8:
        return lax.psum_scatter(pieces, axis, scatter_dimension=0, tiled=False)
    total = lax.dynamic_index_in_dim(pieces, me, 0, keepdims=False)
    for step in range(1, size):
        piece = lax.dynamic_index_in_dim(pieces, (me + step) % size, 0, keepdims=False)
        total = total + lax.ppermute(piece, axis, [(i, (i + step) % size) for i in range(size)])
    return total


def shards(query_input, key_input, value_input, filters, complement, doc_lengths, cotangent):
    channels, taps = filters.shape
    ctx, ch = lax.axis_size("ctx"), lax.axis_size("ch")
    up = [(i, i + 1) for i in range(ctx - 1)]
    down = [(j, i) for i, j in up]
    product = (key_input.astype(F32) * value_input.astype(F32)).astype(BF16)
    upstream = (cotangent.astype(F32) * query_input.astype(F32)).astype(BF16)
    halos = [lax.ppermute(field, "ctx", way) for field in (product, upstream) for way in (up, down)]

    place = (lax.axis_index("ch") - complement // channels) % ch * channels + complement % channels
    partner = jnp.take(gather_relative(filters, "ch"), place, axis=0, mode="clip")
    *mixed, tap_sums = mix(
        doc_lengths, (query_input, key_input, value_input, cotangent, *halos), filters, partner, ctx
    )
    share = taps // ctx
    owned = reduce_owned(tap_sums.reshape(ctx, 2 * share, channels), "ctx")
    mirrored = gather_relative(owned[share:].T, "ch")
    grad_filter = owned[:share].T + jnp.take(mirrored, place, axis=0, mode="clip")
    return (*mixed, grad_filter)


def solution(mesh):
    placed = (
        P("ctx", "ch"),
        P("ctx", "ch"),
        P("ctx", "ch"),
        P("ch", None),
        P("ch"),
        P(),
        P("ctx", "ch"),
    )
    return jax.shard_map(
        shards,
        mesh=mesh,
        in_specs=placed,
        out_specs=(P("ctx", "ch"), P("ctx", "ch"), P("ctx", "ch"), P("ctx", "ch"), P("ch", "ctx")),
        check_vma=False,
    )
```

time: 1170 us -> 96.7 us (0.08)
  other arithmetic: 979 us -> 4.46 us
  local copies, waits for them, and re-layouts: 107 us -> 9.81 us
  blocking collectives: 42.3 us -> 0 us
  waiting for transfers between devices: 0.75 us -> 39.3 us
  between operations: 20.7 us -> 0.83 us
  Pallas kernels: 0 us -> 17.6 us
  starting transfers between devices: 10.4 us -> 23.3 us
    convert_element_type x19 -> x2, other arithmetic: 833 us -> 2.69 us  [the longest x1 1.91 us: shards(): product = (key_input.astype(F32) * value_input.astype(F32)).astype(BF16)]
    another operation x259 -> x0, local copies, waits for them, and re-layouts: 84.9 us -> none  [the longest x129 59.3 us: backward_filters(): jnp.stack(mirror_cols, axis=1)]
    reduce_sum x45 -> x0, other arithmetic: 66.1 us -> none  [the longest x23 33.3 us: backward_filters(): jnp.sum(jnp.where(after_mask, upstream_f * later_u, 0.0), axis=0)]
    add x4 -> x3, other arithmetic: 50.5 us -> 1.66 us  [the longest x1 0.97 us: reduce_owned(): total + lax.ppermute(piece, axis, [(i, (i + step) % size) for i in range(...]
    all_gather x1 -> x0, blocking collectives: 42.3 us -> none  [shards(): rc_all = lax.all_gather(tied_rc, 'ch', axis=0, tiled=True)]
    ppermute x4 -> x17, waiting for transfers between devices: 0.01 us -> 39.3 us  [the longest x6 28.5 us: gather_relative(): lax.ppermute(shard, axis, [(i, (i + step) % size) for i in range(size)])]
    concatenate x22 -> x2, other arithmetic: 27.4 us -> 0.1 us  [gather_relative(): return jnp.concatenate(blocks, axis=0)]
    pallas_call x0 -> x1, Pallas kernels: none -> 17.6 us  [mix(): pl.pallas_call(mix_kernel, grid=(channels // block,), in_specs=[pl.BlockS...]
  transfers between devices with their start and end apart: 7 -> 17, of which waited for: 0 -> 10; matrix products, arithmetic and copies ran while one was open for 57% -> 5% of each run, Pallas kernels for 0% -> 0%
where the time goes in v1:
time: 96.7 us; the launch traced here: 95.2 us
  waiting for transfers between devices  39.3 us (41%)
  starting transfers between devices  23.3 us (24%)
  Pallas kernels  17.6 us (18%)
  local copies, waits for them, and re-layouts  9.81 us (10%)
  other arithmetic  4.46 us (5%)
    ppermute x6, waiting for transfers between devices, gather_relative(): lax.ppermute(shard, axis, [(i, (i + step) % size) for i in range(size)])  28.5 us
    pallas_call x1, Pallas kernels, mix(): pl.pallas_call(mix_kernel, grid=(channels // block,), in_specs=[pl.BlockS...  17.6 us
    ppermute x7, waiting for transfers between devices, reduce_owned(): lax.ppermute(piece, axis, [(i, (i + step) % size) for i in range(size)])  10.8 us
    ppermute x6, starting transfers between devices, gather_relative(): lax.ppermute(shard, axis, [(i, (i + step) % size) for i in range(size)])  9.24 us
    ppermute x4, starting transfers between devices, shards(): lax.ppermute(field, 'ctx', way)  7.63 us
    ppermute x7, starting transfers between devices, reduce_owned(): lax.ppermute(piece, axis, [(i, (i + step) % size) for i in range(size)])  6.4 us
    gather x1, local copies, waits for them, and re-layouts, shards(): jnp.take(gather_relative(filters, 'ch'), place, axis=0, mode='clip')  3.52 us
    gather x2, local copies, waits for them, and re-layouts, shards(): jnp.take(mirrored, place, axis=0, mode='clip')  2.63 us
  transfers between devices with their start and end apart: 17, of which 10 were waited for; matrix products, arithmetic and copies ran while one was open for 5% of the time, Pallas kernels for 0%

profile of v1, /device:TPU:0, one launch (start us, length us, event | category | flops | bytes accessed | tf_op | source)
XLA Modules:
  0.0 95.2 jit_solution(12978453488769039261)
XLA Ops:
  0.6 0.0 copy-start
  0.6 0.0 copy-start.2
  0.7 0.0 copy-start.1
  0.7 0.0 copy-start.7
  0.7 1.9 %multiply_convert_fusion.1 = bf16[128,1152]{1,0:T(8,128)(2,1)} fusion(bf16[128,1152]{1,0:T(8,128)(2,1)} %value.1, bf16[128,1152]{1,0:T(8,128)(2,1)} %key.1), kind=kLoop, calls=%fused_computation.4 | loop fusion | flops 589824 | bytes 884736 | tf_op jit(solution)/shard_map/convert_element_type | solution.py:184
  2.6 1.3 %collective-permute-start.1 = (bf16[128,1152]{1,0:T(8,128)(2,1)}, bf16[128,1152]{1,0:T(8,128)(2,1)S(1)}, u32[]{:S(2)}, u32[]{:S(2)}) collective-permute-start(bf16[128,1152]{1,0:T(8,128)(2,1)} %multiply_convert_fusion.1), channel_id=1, source_target_pairs={{4,0},{8,4},{12,8},{16,12},{20,16},{24,20},{28,24},{5,1},{9,5},{13... | collective-permute-start | bytes 884744 | tf_op jit(solution)/shard_map/ppermute | solution.py:186
  3.9 3.0 %collective-permute-start = (bf16[128,1152]{1,0:T(8,128)(2,1)}, bf16[128,1152]{1,0:T(8,128)(2,1)S(1)}, u32[]{:S(2)}, u32[]{:S(2)}) collective-permute-start(bf16[128,1152]{1,0:T(8,128)(2,1)} %multiply_convert_fusion.1), channel_id=1, source_target_pairs={{0,4},{4,8},{8,12},{12,16},{16,20},{20,24},{24,28},{1,5},{5,9},{9,... | collective-permute-start | bytes 884744 | tf_op jit(solution)/shard_map/ppermute | solution.py:186
  6.9 5.1 %collective-permute-start.6 = (bf16[1152,128]{1,0:T(8,128)(2,1)}, bf16[1152,128]{1,0:T(8,128)(2,1)S(1)}, u32[]{:S(2)}, u32[]{:S(2)}) collective-permute-start(bf16[1152,128]{1,0:T(8,128)(2,1)} %taps_own.1), channel_id=1, source_target_pairs={{0,3},{1,0},{2,1},{3,2},{4,7},{5,4},{6,5},{7,6},{8,11},{9,8},{10,9... | collective-permute-start | bytes 884744 | tf_op jit(solution)/shard_map/ppermute | solution.py:163
  12.1 0.0 collective-permute-start.5
  12.1 1.0 %collective-permute-start.4 = (bf16[1152,128]{1,0:T(8,128)(2,1)}, bf16[1152,128]{1,0:T(8,128)(2,1)S(1)}, u32[]{:S(2)}, u32[]{:S(2)}) collective-permute-start(bf16[1152,128]{1,0:T(8,128)(2,1)} %taps_own.1), channel_id=1, source_target_pairs={{0,1},{1,2},{2,3},{3,0},{4,5},{5,6},{6,7},{7,4},{8,9},{9,10},{10,1... | collective-permute-start | bytes 884744 | tf_op jit(solution)/shard_map/ppermute | solution.py:163
  13.1 0.0 copy-done.2
  13.1 0.0 copy-done.1
  13.1 0.8 multiply_convert_fusion
  13.9 0.0 copy-done.7
  13.9 5.8 %collective-permute-done.6 = bf16[1152,128]{1,0:T(8,128)(2,1)S(1)} collective-permute-done((bf16[1152,128]{1,0:T(8,128)(2,1)}, bf16[1152,128]{1,0:T(8,128)(2,1)S(1)}, u32[]{:S(2)}, u32[]{:S(2)}) %collective-permute-start.6) | collective-permute-done | bytes 294944 | tf_op jit(solution)/shard_map/ppermute | solution.py:163
  19.7 1.3 %collective-permute-start.3 = (bf16[128,1152]{1,0:T(8,128)(2,1)}, bf16[128,1152]{1,0:T(8,128)(2,1)S(1)}, u32[]{:S(2)}, u32[]{:S(2)}) collective-permute-start(bf16[128,1152]{1,0:T(8,128)(2,1)} %multiply_convert_fusion), channel_id=1, source_target_pairs={{4,0},{8,4},{12,8},{16,12},{20,16},{24,20},{28,24},{5,1},{9,5},{13... | collective-permute-start | bytes 884744 | tf_op jit(solution)/shard_map/ppermute | solution.py:186
  21.0 17.4 %collective-permute-done.5 = bf16[1152,128]{1,0:T(8,128)(2,1)S(1)} collective-permute-done((bf16[1152,128]{1,0:T(8,128)(2,1)}, bf16[1152,128]{1,0:T(8,128)(2,1)S(1)}, u32[]{:S(2)}, u32[]{:S(2)}) %collective-permute-start.5) | collective-permute-done | bytes 294944 | tf_op jit(solution)/shard_map/ppermute | solution.py:163
  38.4 2.0 %collective-permute-start.2 = (bf16[128,1152]{1,0:T(8,128)(2,1)}, bf16[128,1152]{1,0:T(8,128)(2,1)S(1)}, u32[]{:S(2)}, u32[]{:S(2)}) collective-permute-start(bf16[128,1152]{1,0:T(8,128)(2,1)} %multiply_convert_fusion), channel_id=1, source_target_pairs={{0,4},{4,8},{8,12},{12,16},{16,20},{20,24},{24,28},{1,5},{5,9},{9,... | collective-permute-start | bytes 884744 | tf_op jit(solution)/shard_map/ppermute | solution.py:186
  40.4 0.0 collective-permute-done.4
  40.4 0.0 copy-done
  40.5 0.1 pad_maximum_fusion
  40.5 3.5 %gather_fusion = bf16[1152,128]{1,0:T(8,128)(2,1)} fusion(bf16[4608,128]{1,0:T(8,128)(2,1)S(1)} %pad_maximum_fusion, s32[2048]{0:T(1024)S(1)} %pad_clamp_fusion), kind=kCustom, calls=%fused_computation | custom fusion | bytes 594432 | tf_op jit(solution)/shard_map/jit(_take)/gather | solution.py:189
  44.1 0.0 collective-permute-done.1.u_next
  44.1 0.0 copy-start.3
  44.1 0.0 collective-permute-done.u_prev
  44.1 0.0 copy-start.4
  44.1 0.0 collective-permute-done.3.r_next
  44.1 0.0 copy-start.5
  44.1 0.0 collective-permute-done.2.r_prev
  44.1 0.7 copy-done.3
  44.8 0.1 copy-done.4
  44.9 0.1 copy-done.5
  45.0 0.0 copy-start.6
  45.0 0.7 copy-done.6
  45.7 17.6 %mix.1 = (bf16[128,1152]{1,0:T(8,128)(2,1)}, bf16[128,1152]{1,0:T(8,128)(2,1)}, bf16[128,1152]{1,0:T(8,128)(2,1)}, bf16[128,1152]{1,0:T(8,128)(2,1)}, f32[256,1152]{1,0:T(8,128)}) custom-call(s32[16]{0:T(128)} %lens.1, bf16[128,1152]{1,0:T(8,128)(2,1)} %query.1, bf16[128,1152]{1,0:T(8,128)(2,1)} %key.1, bf16[128,1152]{1,0:T(8,128)(2,1)} %value.1, ...), custom_call_target="tpu_custom_call" | custom-call | tf_op jit(solution)/shard_map/mix/pallas_call | solution.py:135
  63.3 1.4 %dynamic-slice_bitcast_fusion.6 = (f32[32,1152]{1,0:T(8,128)S(1)}, f32[32,1152]{1,0:T(8,128)S(1)}, f32[32,1152]{1,0:T(8,128)S(1)}, f32[32,1152]{1,0:T(8,128)S(1)...) fusion(f32[8,32,1152]{2,1,0:T(8,128)} %bitcast.35, s32[]{:T(128)S(6)} %select_n.76, ...), kind=kLoop, calls=%fused_computation.19 | loop fusion | bytes 2064412 | tf_op jit(solution)/shard_map/jit(dynamic_index_in_dim)/squeeze | solution.py:174
  64.7 0.6 collective-permute-start.7
  65.3 2.1 %collective-permute-start.13 = (f32[32,1152]{1,0:T(8,128)S(1)}, f32[32,1152]{1,0:T(8,128)S(1)}, u32[]{:S(2)}, u32[]{:S(2)}) collective-permute-start(f32[32,1152]{1,0:T(8,128)S(1)} %get-tuple-element.31), channel_id=1, source_target_pairs={{0,28},{4,0},{8,4},{12,8},{16,12},{20,16},{24,20},{28,24},{1,29},{... | collective-permute-start | bytes 442376 | tf_op jit(solution)/shard_map/ppermute | solution.py:175
  67.4 1.7 %collective-permute-start.12 = (f32[32,1152]{1,0:T(8,128)S(1)}, f32[32,1152]{1,0:T(8,128)S(1)}, u32[]{:S(2)}, u32[]{:S(2)}) collective-permute-start(f32[32,1152]{1,0:T(8,128)S(1)} %get-tuple-element.32), channel_id=1, source_target_pairs={{0,24},{4,28},{8,0},{12,4},{16,8},{20,12},{24,16},{28,20},{1,25},{... | collective-permute-start | bytes 442376 | tf_op jit(solution)/shard_map/ppermute | solution.py:175
  69.1 0.0 collective-permute-start.11
  69.1 0.2 collective-permute-start.10
  69.3 0.9 collective-permute-done.7
  70.2 0.7 collective-permute-start.9
  70.9 0.8 collective-permute-done.13
  71.6 1.1 %collective-permute-start.8 = (f32[32,1152]{1,0:T(8,128)S(1)}, f32[32,1152]{1,0:T(8,128)S(1)}, u32[]{:S(2)}, u32[]{:S(2)}) collective-permute-start(f32[32,1152]{1,0:T(8,128)S(1)} %get-tuple-element.36), channel_id=1, source_target_pairs={{0,8},{4,12},{8,16},{12,20},{16,24},{20,28},{24,0},{28,4},{1,9},{5... | collective-permute-start | bytes 442376 | tf_op jit(solution)/shard_map/ppermute | solution.py:175
  72.8 1.8 %collective-permute-done.12 = f32[32,1152]{1,0:T(8,128)S(1)} collective-permute-done((f32[32,1152]{1,0:T(8,128)S(1)}, f32[32,1152]{1,0:T(8,128)S(1)}, u32[]{:S(2)}, u32[]{:S(2)}) %collective-permute-start.12) | collective-permute-done | bytes 147488 | tf_op jit(solution)/shard_map/ppermute | solution.py:175
  74.5 0.6 collective-permute-done.11
  75.2 5.2 %collective-permute-done.10 = f32[32,1152]{1,0:T(8,128)S(1)} collective-permute-done((f32[32,1152]{1,0:T(8,128)S(1)}, f32[32,1152]{1,0:T(8,128)S(1)}, u32[]{:S(2)}, u32[]{:S(2)}) %collective-permute-start.10) | collective-permute-done | bytes 147488 | tf_op jit(solution)/shard_map/ppermute | solution.py:175
  80.4 1.5 %collective-permute-done.9 = f32[32,1152]{1,0:T(8,128)S(1)} collective-permute-done((f32[32,1152]{1,0:T(8,128)S(1)}, f32[32,1152]{1,0:T(8,128)S(1)}, u32[]{:S(2)}, u32[]{:S(2)}) %collective-permute-start.9) | collective-permute-done | bytes 147488 | tf_op jit(solution)/shard_map/ppermute | solution.py:175
  81.9 0.0 collective-permute-done.8
  81.9 1.0 %fusion.5 = f32[32,1152]{1,0:T(8,128)S(1)} fusion(f32[32,1152]{1,0:T(8,128)S(1)} %collective-permute-done.13, f32[32,1152]{1,0:T(8,128)S(1)} %collective-permute-done.12, f32[32,1152]{1,0:T(8,128)S(1)} %collective-permute-done.11, f32[32,1152]{1,0:T(8,128)S(1)} %collective-permute-done.10, f32[32,1152]{1,0:T(8,128)S(1)} %collective-permute-done.9, ...), kind=kLoop, calls=%fused_computation.12 | loop fusion | flops 258048 | bytes 1327108 | tf_op jit(solution)/shard_map/add | solution.py:175
  82.9 0.1 collective-permute-start.16
  82.9 1.1 %collective-permute-start.15 = (f32[1152,16]{0,1:T(8,128)S(1)}, f32[1152,16]{0,1:T(8,128)S(1)}, u32[]{:S(2)}, u32[]{:S(2)}) collective-permute-start(f32[1152,16]{0,1:T(8,128)S(1)} %slice_bitcast_fusion), channel_id=1, source_target_pairs={{0,2},{1,3},{2,0},{3,1},{4,6},{5,7},{6,4},{7,5},{8,10},{9,11},{10,... | collective-permute-start | bytes 221192 | tf_op jit(solution)/shard_map/ppermute | solution.py:163
  84.0 1.9 %collective-permute-start.14 = (f32[1152,16]{0,1:T(8,128)S(1)}, f32[1152,16]{0,1:T(8,128)S(1)}, u32[]{:S(2)}, u32[]{:S(2)}) collective-permute-start(f32[1152,16]{0,1:T(8,128)S(1)} %slice_bitcast_fusion), channel_id=1, source_target_pairs={{0,1},{1,2},{2,3},{3,0},{4,5},{5,6},{6,7},{7,4},{8,9},{9,10},{10,1... | collective-permute-start | bytes 221192 | tf_op jit(solution)/shard_map/ppermute | solution.py:163
  86.0 2.2 %collective-permute-done.16 = f32[1152,16]{0,1:T(8,128)S(1)} collective-permute-done((f32[1152,16]{0,1:T(8,128)S(1)}, f32[1152,16]{0,1:T(8,128)S(1)}, u32[]{:S(2)}, u32[]{:S(2)}) %collective-permute-start.16) | collective-permute-done | bytes 73760 | tf_op jit(solution)/shard_map/ppermute | solution.py:163
  88.2 3.1 %collective-permute-done.15 = f32[1152,16]{0,1:T(8,128)S(1)} collective-permute-done((f32[1152,16]{0,1:T(8,128)S(1)}, f32[1152,16]{0,1:T(8,128)S(1)}, u32[]{:S(2)}, u32[]{:S(2)}) %collective-permute-start.15) | collective-permute-done | bytes 73760 | tf_op jit(solution)/shard_map/ppermute | solution.py:163
  91.2 0.0 collective-permute-done.14
  91.3 0.7 copy.58
  91.9 2.4 %gather_fusion.1 = f32[1152,16]{1,0:T(8,128)S(1)} fusion(f32[4608,16]{1,0:T(8,128)S(1)} %copy.58, s32[2048]{0:T(1024)S(1)} %pad_clamp_fusion), kind=kCustom, calls=%fused_computation.1 | custom fusion | bytes 152064 | tf_op jit(solution)/shard_map/jit(_take)/gather | solution.py:196
  94.4 0.2 copy.59
  94.6 0.7 fusion.6
  (4 shorter events, 0.1 us)
Async XLA Ops:
  0.6 39.8 %copy-start = (bf16[1152,128]{1,0:T(8,128)(2,1)S(1)}, bf16[1152,128]{1,0:T(8,128)(2,1)}, u32[]{:S(2)}) copy-start(bf16[1152,128]{1,0:T(8,128)(2,1)} %taps_own.1) | copy-start | bytes 884740
  0.6 12.4 %copy-start.2 = (bf16[128,1152]{1,0:T(8,128)(2,1)S(1)}, bf16[128,1152]{1,0:T(8,128)(2,1)}, u32[]{:S(2)}) copy-start(bf16[128,1152]{1,0:T(8,128)(2,1)} %cot.1) | copy-start | bytes 884740
  0.7 12.4 %copy-start.1 = (bf16[128,1152]{1,0:T(8,128)(2,1)S(1)}, bf16[128,1152]{1,0:T(8,128)(2,1)}, u32[]{:S(2)}) copy-start(bf16[128,1152]{1,0:T(8,128)(2,1)} %query.1) | copy-start | bytes 884740
  0.7 13.2 %copy-start.7 = (s32[1152]{0:T(1024)S(1)}, s32[1152]{0:T(1024)}, u32[]{:S(2)}) copy-start(s32[1152]{0:T(1024)} %param.19) | copy-start | bytes 13828
  2.6 41.5 %collective-permute-start.1 = (bf16[128,1152]{1,0:T(8,128)(2,1)}, bf16[128,1152]{1,0:T(8,128)(2,1)S(1)}, u32[]{:S(2)}, u32[]{:S(2)}) collective-permute-start(bf16[128,1152]{1,0:T(8,128)(2,1)} %multiply_convert_fusion.1), channel_id=1, source_target_pairs={{4,0},{8,4},{12,8},{16,12},{20,16},{24,20},{28,24},{5,1},{9,5},{13... | collective-permute-start | bytes 884744 | tf_op jit(solution)/shard_map/ppermute | solution.py:186
  3.9 40.2 %collective-permute-start = (bf16[128,1152]{1,0:T(8,128)(2,1)}, bf16[128,1152]{1,0:T(8,128)(2,1)S(1)}, u32[]{:S(2)}, u32[]{:S(2)}) collective-permute-start(bf16[128,1152]{1,0:T(8,128)(2,1)} %multiply_convert_fusion.1), channel_id=1, source_target_pairs={{0,4},{4,8},{8,12},{12,16},{16,20},{20,24},{24,28},{1,5},{5,9},{9,... | collective-permute-start | bytes 884744 | tf_op jit(solution)/shard_map/ppermute | solution.py:186
  6.9 12.8 %collective-permute-start.6 = (bf16[1152,128]{1,0:T(8,128)(2,1)}, bf16[1152,128]{1,0:T(8,128)(2,1)S(1)}, u32[]{:S(2)}, u32[]{:S(2)}) collective-permute-start(bf16[1152,128]{1,0:T(8,128)(2,1)} %taps_own.1), channel_id=1, source_target_pairs={{0,3},{1,0},{2,1},{3,2},{4,7},{5,4},{6,5},{7,6},{8,11},{9,8},{10,9... | collective-permute-start | bytes 884744 | tf_op jit(solution)/shard_map/ppermute | solution.py:163
  12.1 26.3 %collective-permute-start.5 = (bf16[1152,128]{1,0:T(8,128)(2,1)}, bf16[1152,128]{1,0:T(8,128)(2,1)S(1)}, u32[]{:S(2)}, u32[]{:S(2)}) collective-permute-start(bf16[1152,128]{1,0:T(8,128)(2,1)} %taps_own.1), channel_id=1, source_target_pairs={{0,2},{1,3},{2,0},{3,1},{4,6},{5,7},{6,4},{7,5},{8,10},{9,11},{10,... | collective-permute-start | bytes 884744 | tf_op jit(solution)/shard_map/ppermute | solution.py:163
  12.1 28.4 %collective-permute-start.4 = (bf16[1152,128]{1,0:T(8,128)(2,1)}, bf16[1152,128]{1,0:T(8,128)(2,1)S(1)}, u32[]{:S(2)}, u32[]{:S(2)}) collective-permute-start(bf16[1152,128]{1,0:T(8,128)(2,1)} %taps_own.1), channel_id=1, source_target_pairs={{0,1},{1,2},{2,3},{3,0},{4,5},{5,6},{6,7},{7,4},{8,9},{9,10},{10,1... | collective-permute-start | bytes 884744 | tf_op jit(solution)/shard_map/ppermute | solution.py:163
  19.7 24.3 %collective-permute-start.3 = (bf16[128,1152]{1,0:T(8,128)(2,1)}, bf16[128,1152]{1,0:T(8,128)(2,1)S(1)}, u32[]{:S(2)}, u32[]{:S(2)}) collective-permute-start(bf16[128,1152]{1,0:T(8,128)(2,1)} %multiply_convert_fusion), channel_id=1, source_target_pairs={{4,0},{8,4},{12,8},{16,12},{20,16},{24,20},{28,24},{5,1},{9,5},{13... | collective-permute-start | bytes 884744 | tf_op jit(solution)/shard_map/ppermute | solution.py:186
  38.4 5.7 %collective-permute-start.2 = (bf16[128,1152]{1,0:T(8,128)(2,1)}, bf16[128,1152]{1,0:T(8,128)(2,1)S(1)}, u32[]{:S(2)}, u32[]{:S(2)}) collective-permute-start(bf16[128,1152]{1,0:T(8,128)(2,1)} %multiply_convert_fusion), channel_id=1, source_target_pairs={{0,4},{4,8},{8,12},{12,16},{16,20},{20,24},{24,28},{1,5},{5,9},{9,... | collective-permute-start | bytes 884744 | tf_op jit(solution)/shard_map/ppermute | solution.py:186
  44.1 0.7 copy-start.3
  44.1 0.8 copy-start.4
  44.1 0.9 copy-start.5
  45.0 0.7 copy-start.6
  64.7 5.5 %collective-permute-start.7 = (f32[32,1152]{1,0:T(8,128)S(1)}, f32[32,1152]{1,0:T(8,128)S(1)}, u32[]{:S(2)}, u32[]{:S(2)}) collective-permute-start(f32[32,1152]{1,0:T(8,128)S(1)} %get-tuple-element.30), channel_id=1, source_target_pairs={{0,4},{4,8},{8,12},{12,16},{16,20},{20,24},{24,28},{28,0},{1,5},{5... | collective-permute-start | bytes 442376 | tf_op jit(solution)/shard_map/ppermute | solution.py:175
  65.3 6.3 %collective-permute-start.13 = (f32[32,1152]{1,0:T(8,128)S(1)}, f32[32,1152]{1,0:T(8,128)S(1)}, u32[]{:S(2)}, u32[]{:S(2)}) collective-permute-start(f32[32,1152]{1,0:T(8,128)S(1)} %get-tuple-element.31), channel_id=1, source_target_pairs={{0,28},{4,0},{8,4},{12,8},{16,12},{20,16},{24,20},{28,24},{1,29},{... | collective-permute-start | bytes 442376 | tf_op jit(solution)/shard_map/ppermute | solution.py:175
  67.4 7.2 %collective-permute-start.12 = (f32[32,1152]{1,0:T(8,128)S(1)}, f32[32,1152]{1,0:T(8,128)S(1)}, u32[]{:S(2)}, u32[]{:S(2)}) collective-permute-start(f32[32,1152]{1,0:T(8,128)S(1)} %get-tuple-element.32), channel_id=1, source_target_pairs={{0,24},{4,28},{8,0},{12,4},{16,8},{20,12},{24,16},{28,20},{1,25},{... | collective-permute-start | bytes 442376 | tf_op jit(solution)/shard_map/ppermute | solution.py:175
  69.1 6.1 %collective-permute-start.11 = (f32[32,1152]{1,0:T(8,128)S(1)}, f32[32,1152]{1,0:T(8,128)S(1)}, u32[]{:S(2)}, u32[]{:S(2)}) collective-permute-start(f32[32,1152]{1,0:T(8,128)S(1)} %get-tuple-element.33), channel_id=1, source_target_pairs={{0,20},{4,24},{8,28},{12,0},{16,4},{20,8},{24,12},{28,16},{1,21},{... | collective-permute-start | bytes 442376 | tf_op jit(solution)/shard_map/ppermute | solution.py:175
  69.1 11.3 %collective-permute-start.10 = (f32[32,1152]{1,0:T(8,128)S(1)}, f32[32,1152]{1,0:T(8,128)S(1)}, u32[]{:S(2)}, u32[]{:S(2)}) collective-permute-start(f32[32,1152]{1,0:T(8,128)S(1)} %get-tuple-element.34), channel_id=1, source_target_pairs={{0,16},{4,20},{8,24},{12,28},{16,0},{20,4},{24,8},{28,12},{1,17},{... | collective-permute-start | bytes 442376 | tf_op jit(solution)/shard_map/ppermute | solution.py:175
  70.2 11.7 %collective-permute-start.9 = (f32[32,1152]{1,0:T(8,128)S(1)}, f32[32,1152]{1,0:T(8,128)S(1)}, u32[]{:S(2)}, u32[]{:S(2)}) collective-permute-start(f32[32,1152]{1,0:T(8,128)S(1)} %get-tuple-element.35), channel_id=1, source_target_pairs={{0,12},{4,16},{8,20},{12,24},{16,28},{20,0},{24,4},{28,8},{1,13},{... | collective-permute-start | bytes 442376 | tf_op jit(solution)/shard_map/ppermute | solution.py:175
  71.6 10.2 %collective-permute-start.8 = (f32[32,1152]{1,0:T(8,128)S(1)}, f32[32,1152]{1,0:T(8,128)S(1)}, u32[]{:S(2)}, u32[]{:S(2)}) collective-permute-start(f32[32,1152]{1,0:T(8,128)S(1)} %get-tuple-element.36), channel_id=1, source_target_pairs={{0,8},{4,12},{8,16},{12,20},{16,24},{20,28},{24,0},{28,4},{1,9},{5... | collective-permute-start | bytes 442376 | tf_op jit(solution)/shard_map/ppermute | solution.py:175
  82.9 5.3 %collective-permute-start.16 = (f32[1152,16]{0,1:T(8,128)S(1)}, f32[1152,16]{0,1:T(8,128)S(1)}, u32[]{:S(2)}, u32[]{:S(2)}) collective-permute-start(f32[1152,16]{0,1:T(8,128)S(1)} %slice_bitcast_fusion), channel_id=1, source_target_pairs={{0,3},{1,0},{2,1},{3,2},{4,7},{5,4},{6,5},{7,6},{8,11},{9,8},{10,9... | collective-permute-start | bytes 221192 | tf_op jit(solution)/shard_map/ppermute | solution.py:163
  82.9 8.3 %collective-permute-start.15 = (f32[1152,16]{0,1:T(8,128)S(1)}, f32[1152,16]{0,1:T(8,128)S(1)}, u32[]{:S(2)}, u32[]{:S(2)}) collective-permute-start(f32[1152,16]{0,1:T(8,128)S(1)} %slice_bitcast_fusion), channel_id=1, source_target_pairs={{0,2},{1,3},{2,0},{3,1},{4,6},{5,7},{6,4},{7,5},{8,10},{9,11},{10,... | collective-permute-start | bytes 221192 | tf_op jit(solution)/shard_map/ppermute | solution.py:163
  84.0 7.2 %collective-permute-start.14 = (f32[1152,16]{0,1:T(8,128)S(1)}, f32[1152,16]{0,1:T(8,128)S(1)}, u32[]{:S(2)}, u32[]{:S(2)}) collective-permute-start(f32[1152,16]{0,1:T(8,128)S(1)} %slice_bitcast_fusion), channel_id=1, source_target_pairs={{0,1},{1,2},{2,3},{3,0},{4,5},{5,6},{6,7},{7,4},{8,9},{9,10},{10,1... | collective-permute-start | bytes 221192 | tf_op jit(solution)/shard_map/ppermute | solution.py:163

commit v2 on v1

--- a/solution.py
+++ b/solution.py
@@ -113,7 +113,8 @@
     g_sum = acc_g[...]
     g_hi = g_sum.astype(BF16)
     g_lo = (g_sum - g_hi.astype(F32)).astype(BF16)
-    tap_sums[...] = mm(tap_hi[...], g_hi) + mm(tap_hi[...], g_lo) + mm(tap_lo[...], g_hi)
+    sums = mm(tap_hi[...], g_hi) + mm(tap_hi[...], g_lo) + mm(tap_lo[...], g_hi)
+    tap_sums[...] = sums.astype(BF16)
 
 
 def channel_block(channels):
@@ -141,7 +142,7 @@
         + table_specs,
         out_specs=[field_spec] * 4 + [pl.BlockSpec((2 * taps, block), lambda i: (0, i))],
         out_shape=[jax.ShapeDtypeStruct((rows, channels), BF16)] * 4
-        + [jax.ShapeDtypeStruct((2 * taps, channels), F32)],
+        + [jax.ShapeDtypeStruct((2 * taps, channels), BF16)],
         scratch_shapes=[
             pltpu.VMEM((length, block), F32),
             pltpu.VMEM((length, block), BF16),
@@ -156,44 +157,148 @@
     )(doc_lengths, *fields, filters, partner, *[jnp.asarray(t) for t in tables])
 
 
-def gather_relative(shard, axis):
-    size = lax.axis_size(axis)
-    blocks = [shard]
-    for step in range(1, size):
-        blocks.append(lax.ppermute(shard, axis, [(i, (i + step) % size) for i in range(size)]))
-    return jnp.concatenate(blocks, axis=0)
-
-
-def reduce_owned(pieces, axis):
-    size = lax.axis_size(axis)
-    me = lax.axis_index(axis)
-    if size > 8:
-        return lax.psum_scatter(pieces, axis, scatter_dimension=0, tiled=False)
-    total = lax.dynamic_index_in_dim(pieces, me, 0, keepdims=False)
-    for step in range(1, size):
-        piece = lax.dynamic_index_in_dim(pieces, (me + step) % size, 0, keepdims=False)
-        total = total + lax.ppermute(piece, axis, [(i, (i + step) % size) for i in range(size)])
-    return total
+def remote(src, dst, sems, index, device):
+    return pltpu.make_async_remote_copy(
+        src_ref=src, dst_ref=dst, send_sem=sems[0].at[index], recv_sem=sems[1].at[index],
+        device_id=device, device_id_type=pl.DeviceIdType.MESH,
+    )
+
+
+def greet(devices):
+    barrier = pltpu.get_barrier_semaphore()
+    for device in devices:
+        pl.semaphore_signal(barrier, inc=1, device_id=device, device_id_type=pl.DeviceIdType.MESH)
+    pl.semaphore_wait(barrier, len(devices))
+
+
+def spread_kernel(ctx, ch, u, r, filters, u_prev, u_next, r_prev, r_next, gathered,
+                  halo_send, halo_recv, ch_send, ch_recv, core_send, core_recv, local):
+    me, mine = lax.axis_index("ctx"), lax.axis_index("ch")
+    after, before = {"ctx": (me + 1) % ctx}, {"ctx": (me + ctx - 1) % ctx}
+    parity = me % 2
+    twin = {"ctx": me + 1 - 2 * parity}
+    rows = filters.shape[0] // 2
+    half = pl.ds(pl.multiple_of(parity * rows, rows), rows)
+    peers = [{"ch": (mine + step) % ch} for step in range(1, ch)]
+    keep = pltpu.make_async_copy(filters, gathered.at[0], local)
+    keep.start()
+    greet([after, before] + peers)
+    wide = [
+        remote(filters.at[half], gathered.at[step, half], (ch_send, ch_recv), step - 1, peers[step - 1])
+        for step in range(1, ch)
+    ]
+    for copy in wide[::-1]:
+        copy.start()
+    halos = [
+        remote(field, place, (halo_send, halo_recv), index, device)
+        for index, (field, place, device) in enumerate(
+            ((u, u_prev, after), (u, u_next, before), (r, r_prev, after), (r, r_next, before))
+        )
+    ]
+    for copy in halos:
+        copy.start()
+    swaps = []
+    for step in range(1, ch):
+        wide[step - 1].wait_recv()
+        swap = remote(gathered.at[step, half], gathered.at[step, half], (core_send, core_recv), step - 1, twin)
+        swap.start()
+        swaps.append(swap)
+    for copy in swaps:
+        copy.wait()
+    for copy in wide:
+        copy.wait_send()
+    for copy in halos:
+        copy.wait()
+    keep.wait()
+
+
+def spread(product, upstream, filters):
+    ctx, ch = lax.axis_size("ctx"), lax.axis_size("ch")
+    hbm = pl.BlockSpec(memory_space=pl.ANY)
+    dma = pltpu.SemaphoreType.DMA
+    field = jax.ShapeDtypeStruct(product.shape, BF16)
+    return pl.pallas_call(
+        functools.partial(spread_kernel, ctx, ch),
+        in_specs=[hbm] * 3,
+        out_specs=[hbm] * 5,
+        out_shape=[field] * 4 + [jax.ShapeDtypeStruct((ch, *filters.shape), BF16)],
+        scratch_shapes=[dma((4,)), dma((4,)), dma((ch - 1,)), dma((ch - 1,)), dma((ch - 1,)), dma((ch - 1,)), dma],
+        compiler_params=pltpu.CompilerParams(collective_id=0, has_side_effects=True),
+        name="spread",
+    )(product, upstream, filters)
+
+
+def collect_kernel(ctx, ch, pieces, own, mirrored, landed, sent, got, sum_send, sum_recv, ch_send, ch_recv, local):
+    me, mine = lax.axis_index("ctx"), lax.axis_index("ch")
+    share = own.shape[0]
+    others = [{"ctx": (me + step) % ctx} for step in range(1, ctx)]
+    peers = [{"ch": (mine + step) % ch} for step in range(1, ch)]
+    keep = pltpu.make_async_copy(pieces.at[me], landed.at[0], local)
+    keep.start()
+    greet(others + peers)
+    copies = [
+        remote(pieces.at[(me + step) % ctx], landed.at[step], (sum_send, sum_recv), step - 1, others[step - 1])
+        for step in range(1, ctx)
+    ]
+    for copy in copies:
+        copy.start()
+    keep.wait()
+    for copy in copies:
+        copy.wait()
+    sent[...] = sum(landed[step, share:].astype(F32) for step in range(ctx)).astype(BF16)
+    own[...] = sum(landed[step, :share].astype(F32) for step in range(ctx))
+    copies = [
+        remote(sent, got.at[step - 1], (ch_send, ch_recv), step - 1, peers[step - 1]) for step in range(1, ch)
+    ]
+    for copy in copies:
+        copy.start()
+    mirrored[0] = sent[...]
+    for step, copy in enumerate(copies):
+        copy.wait()
+        mirrored[step + 1] = got[step]
+
+
+def collect(pieces):
+    ctx, ch = lax.axis_size("ctx"), lax.axis_size("ch")
+    _, double, channels = pieces.shape
+    share = double // 2
+    vmem = pl.BlockSpec(memory_space=pltpu.VMEM)
+    dma = pltpu.SemaphoreType.DMA
+    return pl.pallas_call(
+        functools.partial(collect_kernel, ctx, ch),
+        in_specs=[pl.BlockSpec(memory_space=pl.ANY)],
+        out_specs=[vmem] * 2,
+        out_shape=[
+            jax.ShapeDtypeStruct((share, channels), F32),
+            jax.ShapeDtypeStruct((ch, share, channels), BF16),
+        ],
+        scratch_shapes=[
+            pltpu.VMEM((ctx, double, channels), BF16),
+            pltpu.VMEM((share, channels), BF16),
+            pltpu.VMEM((ch - 1, share, channels), BF16),
+            dma((ctx - 1,)), dma((ctx - 1,)), dma((ch - 1,)), dma((ch - 1,)), dma,
+        ],
+        compiler_params=pltpu.CompilerParams(collective_id=1, has_side_effects=True),
+        name="collect",
+    )(pieces)
 
 
 def shards(query_input, key_input, value_input, filters, complement, doc_lengths, cotangent):
     channels, taps = filters.shape
     ctx, ch = lax.axis_size("ctx"), lax.axis_size("ch")
-    up = [(i, i + 1) for i in range(ctx - 1)]
-    down = [(j, i) for i, j in up]
     product = (key_input.astype(F32) * value_input.astype(F32)).astype(BF16)
     upstream = (cotangent.astype(F32) * query_input.astype(F32)).astype(BF16)
-    halos = [lax.ppermute(field, "ctx", way) for field in (product, upstream) for way in (up, down)]
+    *halos, gathered = spread(product, upstream, filters)
 
     place = (lax.axis_index("ch") - complement // channels) % ch * channels + complement % channels
-    partner = jnp.take(gather_relative(filters, "ch"), place, axis=0, mode="clip")
+    partner = jnp.take(gathered.reshape(ch * channels, taps), place, axis=0, mode="clip")
     *mixed, tap_sums = mix(
         doc_lengths, (query_input, key_input, value_input, cotangent, *halos), filters, partner, ctx
     )
     share = taps // ctx
-    owned = reduce_owned(tap_sums.reshape(ctx, 2 * share, channels), "ctx")
-    mirrored = gather_relative(owned[share:].T, "ch")
-    grad_filter = owned[:share].T + jnp.take(mirrored, place, axis=0, mode="clip")
+    own, mirrored = collect(tap_sums.reshape(ctx, 2 * share, channels))
+    mirrored = jnp.swapaxes(mirrored, 1, 2).reshape(ch * channels, share)
+    grad_filter = own.T + jnp.take(mirrored, place, axis=0, mode="clip").astype(F32)
     return (*mixed, grad_filter)
 
 

time: 96.7 us -> 67.9 us (0.70); the launches traced: 95.2 us -> 69.2 us
  waiting for transfers between devices: 39.3 us -> 0 us
  Pallas kernels: 17.6 us -> 55.8 us
  starting transfers between devices: 23.3 us -> 0 us
    pallas_call x0 -> x2, Pallas kernels: none -> 43.7 us  [the longest x1 22.4 us: collect(): pl.pallas_call(functools.partial(collect_kernel, ctx, ch), in_specs=[pl.B...]
    ppermute x17 -> x0, waiting for transfers between devices: 39.3 us -> none  [the longest x6 28.5 us: gather_relative(): lax.ppermute(shard, axis, [(i, (i + step) % size) for i in range(size)])]
    ppermute x17 -> x0, starting transfers between devices: 23.3 us -> none  [the longest x6 9.24 us: gather_relative(): lax.ppermute(shard, axis, [(i, (i + step) % size) for i in range(size)])]
    pallas_call x1, Pallas kernels: 17.6 us -> 12.1 us  [mix(): pl.pallas_call(mix_kernel, grid=(channels // block,), in_specs=[pl.BlockS...]
    convert_element_type x1 -> x0, other arithmetic: 1.91 us -> none  [shards(): product = (key_input.astype(F32) * value_input.astype(F32)).astype(BF16)]
    unnamed x16 -> x2, local copies, waits for them, and re-layouts: 1.62 us -> 0.01 us
    gather x3, local copies, waits for them, and re-layouts: 6.14 us -> 7.64 us  [the longest x1 4.57 us: shards(): jnp.take(gathered.reshape(ch * channels, taps), place, axis=0, mode='clip')]
    reshape x0 -> x1, local copies, waits for them, and re-layouts: none -> 1.43 us  [shards(): mirrored = jnp.swapaxes(mirrored, 1, 2).reshape(ch * channels, share)]
  transfers between devices with their start and end apart: 17 -> 0, of which waited for: 10 -> 0; matrix products, arithmetic and copies ran while one was open for 5% -> 0% of each run, Pallas kernels for 0% -> 0%
where the time goes in v2:
time: 67.9 us; the launch traced here: 69.2 us
  Pallas kernels  55.8 us (82%)
  local copies, waits for them, and re-layouts  9.08 us (13%)
  other arithmetic  3.57 us (5%)
  between operations  0.69 us (1%)
    pallas_call x1, Pallas kernels, collect(): pl.pallas_call(functools.partial(collect_kernel, ctx, ch), in_specs=[pl.B...  22.4 us
    pallas_call x1, Pallas kernels, spread(): pl.pallas_call(functools.partial(spread_kernel, ctx, ch), in_specs=[hbm]...  21.2 us
    pallas_call x1, Pallas kernels, mix(): pl.pallas_call(mix_kernel, grid=(channels // block,), in_specs=[pl.BlockS...  12.1 us
    gather x1, local copies, waits for them, and re-layouts, shards(): jnp.take(gathered.reshape(ch * channels, taps), place, axis=0, mode='clip')  4.57 us
    gather x2, local copies, waits for them, and re-layouts, shards(): jnp.take(mirrored, place, axis=0, mode='clip').astype(F32)  3.07 us
    convert_element_type x1, other arithmetic, shards(): upstream = (cotangent.astype(F32) * query_input.astype(F32)).astype(BF16)  2.18 us
    reshape x1, local copies, waits for them, and re-layouts, shards(): mirrored = jnp.swapaxes(mirrored, 1, 2).reshape(ch * channels, share)  1.43 us

profile of v2, /device:TPU:0, one launch (start us, length us, event | category | flops | bytes accessed | tf_op | source)
XLA Modules:
  0.0 69.2 jit_solution(7687877256898101829)
XLA Ops:
  0.6 0.7 %fusion.3 = s32[1152]{0:T(1024)S(1)} fusion(s32[1152]{0:T(1024)} %param.19, s32[]{:T(128)S(6)} %axis_index.12), kind=kLoop, calls=%fused_computation.13 | loop fusion | flops 29952 | bytes 9220 | tf_op jit(solution)/shard_map/add | solution.py:293
  1.4 2.2 %multiply_convert_fusion = (bf16[128,1152]{1,0:T(8,128)(2,1)}, bf16[128,1152]{1,0:T(8,128)(2,1)}) fusion(bf16[128,1152]{1,0:T(8,128)(2,1)} %query.1, bf16[128,1152]{1,0:T(8,128)(2,1)} %cot.1, bf16[128,1152]{1,0:T(8,128)(2,1)} %value.1, bf16[128,1152]{1,0:T(8,128)(2,1)} %key.1), kind=kLoop, calls=%fused_computation.2 | loop fusion | flops 1179648 | bytes 1769472 | tf_op jit(solution)/shard_map/convert_element_type | solution.py:290
  3.6 21.2 %spread.1 = (bf16[128,1152]{1,0:T(8,128)(2,1)}, bf16[128,1152]{1,0:T(8,128)(2,1)}, bf16[128,1152]{1,0:T(8,128)(2,1)}, bf16[128,1152]{1,0:T(8,128)(2,1)}, bf16[4,1152,128]{2,1,0:T(8,128)(2,1)}) custom-call(bf16[128,1152]{1,0:T(8,128)(2,1)} %get-tuple-element.30.u, bf16[128,1152]{1,0:T(8,128)(2,1)} %get-tuple-element.29.r, bf16[1152,128]{1,0:T(8,128)(2,1)} %taps_own.1), custom_call_target="tpu_custom_call" | custom-call | tf_op jit(solution)/shard_map/spread/pallas_call | solution.py:220
  24.8 4.6 %gather_fusion = bf16[1152,128]{1,0:T(8,128)(2,1)} fusion(bf16[4608,128]{1,0:T(8,128)(2,1)} %bitcast.7, s32[2048]{0:T(1024)S(1)} %pad_clamp_fusion), kind=kCustom, calls=%fused_computation | custom fusion | bytes 594432 | tf_op jit(solution)/shard_map/jit(_take)/gather | solution.py:294
  29.4 12.1 %mix.1 = (bf16[128,1152]{1,0:T(8,128)(2,1)}, bf16[128,1152]{1,0:T(8,128)(2,1)}, bf16[128,1152]{1,0:T(8,128)(2,1)}, bf16[128,1152]{1,0:T(8,128)(2,1)}, bf16[256,1152]{1,0:T(8,128)(2,1)}) custom-call(s32[16]{0:T(128)} %lens.1, bf16[128,1152]{1,0:T(8,128)(2,1)} %query.1, bf16[128,1152]{1,0:T(8,128)(2,1)} %key.1, bf16[128,1152]{1,0:T(8,128)(2,1)} %value.1, ...), custom_call_target="tpu_custom_call" | custom-call | tf_op jit(solution)/shard_map/mix/pallas_call | solution.py:136
  41.5 22.4 %collect.1 = (f32[16,1152]{1,0:T(8,128)}, bf16[4,16,1152]{2,1,0:T(8,128)(2,1)}) custom-call(bf16[8,32,1152]{2,1,0:T(8,128)(2,1)} %bitcast.8), custom_call_target="tpu_custom_call" | custom-call | tf_op jit(solution)/shard_map/collect/pallas_call | solution.py:267
  64.0 1.4 %copy.24 = bf16[4,1152,16]{2,1,0:T(8,128)(2,1)S(1)} copy(bf16[4,1152,16]{1,2,0:T(8,128)(2,1)} %bitcast.9) | data formatting | bytes 294912 | tf_op jit(solution)/shard_map/reshape | solution.py:300
  65.4 0.0 copy-start
  65.4 2.9 %gather_fusion.1 = bf16[1152,16]{1,0:T(8,128)(2,1)S(1)} fusion(bf16[4608,16]{1,0:T(8,128)(2,1)S(1)} %bitcast.6, s32[2048]{0:T(1024)S(1)} %pad_clamp_fusion), kind=kCustom, calls=%fused_computation.1 | custom fusion | bytes 78336 | tf_op jit(solution)/shard_map/jit(_take)/gather | solution.py:301
  68.4 0.1 copy.23
  68.5 0.0 copy-done
  68.5 0.7 bitcast_add_fusion
  (1 shorter events, 0.0 us)
Async XLA Ops:
  65.4 3.1 %copy-start = (f32[16,1152]{1,0:T(8,128)S(1)}, f32[16,1152]{1,0:T(8,128)}, u32[]{:S(2)}) copy-start(f32[16,1152]{1,0:T(8,128)} %get-tuple-element.27) | copy-start | bytes 221188

commit v3 on v2

--- a/solution.py
+++ b/solution.py
@@ -20,7 +20,7 @@
 def fourier_tables(rows, taps, owners):
     length = 3 * rows
     angle = 2.0 * np.pi * (np.arange(length // 2) + 0.5) / length
-    places = np.arange(length) - rows
+    places = np.concatenate([np.arange(rows), np.arange(rows) - rows, np.arange(rows) + rows])
     turns = angle[:, None] * places[None, :]
     analyse = np.concatenate([np.cos(turns), -np.sin(turns)], axis=0)
     own = np.arange(rows)[:, None] * angle[None, :]
@@ -56,7 +56,7 @@
     lens, query, key, value, cot, u_prev, u_next, r_prev, r_next, taps_own, taps_partner,
     analyse, rebuild, causal_hi, causal_lo, anti_hi, anti_lo, tap_hi, tap_lo,
     mixer_out, grad_query, grad_key, grad_value, tap_sums,
-    spectrum, window_u, own_r, acc_y, acc_p, acc_g, z_ref, q_ref,
+    spectrum, own_pair, halo_pair, acc, acc_g, pair_hat,
 ):
     rows = query.shape[0]
     half = analyse.shape[0] // 2
@@ -66,12 +66,15 @@
     spectrum[...] = (
         mm_t(causal_hi[...], f) + mm_t(causal_lo[...], f) + mm_t(anti_hi[...], g) + mm_t(anti_lo[...], g)
     )
-    window_u[0:rows] = u_prev[...]
-    window_u[rows : 2 * rows] = (key[...].astype(F32) * value[...].astype(F32)).astype(BF16)
-    window_u[2 * rows : 3 * rows] = u_next[...]
-    own_r[...] = (cot[...].astype(F32) * query[...].astype(F32)).astype(BF16)
-    acc_y[...] = jnp.zeros_like(acc_y)
-    acc_p[...] = jnp.zeros_like(acc_p)
+    block = query.shape[1]
+    left, right = pl.ds(0, block), pl.ds(block, block)
+    own_pair[:, left] = (key[...].astype(F32) * value[...].astype(F32)).astype(BF16)
+    own_pair[:, right] = (cot[...].astype(F32) * query[...].astype(F32)).astype(BF16)
+    halo_pair[:rows, left] = u_prev[...]
+    halo_pair[rows:, left] = u_next[...]
+    halo_pair[:rows, right] = r_prev[...]
+    halo_pair[rows:, right] = r_next[...]
+    acc[...] = jnp.zeros_like(acc)
     acc_g[...] = jnp.zeros_like(acc_g)
 
     def document(d, start):
@@ -80,32 +83,31 @@
         @pl.when((start < first_place + rows) & (end > first_place))
         def _():
             low, high = start - first_place, end - first_place
-            lane = lax.broadcasted_iota(jnp.int32, (1, 3 * rows), 1) - rows
+            lane = lax.broadcasted_iota(jnp.int32, (1, 3 * rows), 1)
+            lane = jnp.where(lane < rows, lane, jnp.where(lane < 2 * rows, lane - 2 * rows, lane - rows))
             here = ((lane >= low) & (lane < high)).astype(F32).astype(BF16)
             masked = analyse[...] * here
             column = lax.broadcasted_iota(jnp.int32, (rows, 1), 0)
             kept = ((column >= low) & (column < high)).astype(F32).astype(BF16)
             back = rebuild[...] * kept
-            u_hat = mm(masked, window_u[...])
-            o_hat = mm(masked[:, rows : 2 * rows], own_r[...])
-            r_hat = o_hat + mm(masked[:, :rows], r_prev[...]) + mm(masked[:, 2 * rows :], r_next[...])
+            own_hat = mm(masked[:, :rows], own_pair[...])
+            hat = own_hat + mm(masked[:, rows:], halo_pair[...])
             h_re, h_im = spectrum[:half], spectrum[half:]
-            u_re, u_im = u_hat[:half], u_hat[half:]
-            r_re, r_im = r_hat[:half], r_hat[half:]
-            o_re, o_im = o_hat[:half], o_hat[half:]
-            z_ref[:half] = (h_re * u_re - h_im * u_im).astype(BF16)
-            z_ref[half:] = (h_re * u_im + h_im * u_re).astype(BF16)
-            q_ref[:half] = (h_re * r_re + h_im * r_im).astype(BF16)
-            q_ref[half:] = (h_re * r_im - h_im * r_re).astype(BF16)
+            u_re, u_im = hat[:half, :block], hat[half:, :block]
+            r_re, r_im = hat[:half, block:], hat[half:, block:]
+            o_re, o_im = own_hat[:half, block:], own_hat[half:, block:]
+            pair_hat[:half, left] = (h_re * u_re - h_im * u_im).astype(BF16)
+            pair_hat[half:, left] = (h_re * u_im + h_im * u_re).astype(BF16)
+            pair_hat[:half, right] = (h_re * r_re + h_im * r_im).astype(BF16)
+            pair_hat[half:, right] = (h_re * r_im - h_im * r_re).astype(BF16)
             acc_g[:half] += o_re * u_re + o_im * u_im
             acc_g[half:] += o_im * u_re - o_re * u_im
-            acc_y[...] += mm(back, z_ref[...])
-            acc_p[...] += mm(back, q_ref[...])
+            acc[...] += mm(back, pair_hat[...])
 
         return end
 
     lax.fori_loop(0, lens.shape[0], document, jnp.int32(0))
-    combined, grad_product = acc_y[...], acc_p[...]
+    combined, grad_product = acc[:, left], acc[:, right]
     mixer_out[...] = (query[...].astype(F32) * combined).astype(BF16)
     grad_query[...] = (cot[...].astype(F32) * combined).astype(BF16)
     grad_key[...] = (grad_product * value[...].astype(F32)).astype(BF16)
@@ -145,13 +147,11 @@
         + [jax.ShapeDtypeStruct((2 * taps, channels), BF16)],
         scratch_shapes=[
             pltpu.VMEM((length, block), F32),
-            pltpu.VMEM((length, block), BF16),
-            pltpu.VMEM((rows, block), BF16),
-            pltpu.VMEM((rows, block), F32),
-            pltpu.VMEM((rows, block), F32),
+            pltpu.VMEM((rows, 2 * block), BF16),
+            pltpu.VMEM((2 * rows, 2 * block), BF16),
+            pltpu.VMEM((rows, 2 * block), F32),
             pltpu.VMEM((length, block), F32),
-            pltpu.VMEM((length, block), BF16),
-            pltpu.VMEM((length, block), BF16),
+            pltpu.VMEM((length, 2 * block), BF16),
         ],
         name="mix",
     )(doc_lengths, *fields, filters, partner, *[jnp.asarray(t) for t in tables])

time: 67.9 us -> 69.1 us (1.018)
  Pallas kernels: 55.8 us -> 56.5 us
    pallas_call x1, Pallas kernels: 22.4 us -> 25.8 us  [collect(): pl.pallas_call(functools.partial(collect_kernel, ctx, ch), in_specs=[pl.B...]
    pallas_call x1, Pallas kernels: 12.1 us -> 9.52 us  [mix(): pl.pallas_call(mix_kernel, grid=(channels // block,), in_specs=[pl.BlockS...]
where the time goes in v3:
time: 69.1 us; the launch traced here: 69.8 us
  Pallas kernels  56.5 us (82%)
  local copies, waits for them, and re-layouts  9.08 us (13%)
  other arithmetic  3.57 us (5%)
    pallas_call x1, Pallas kernels, collect(): pl.pallas_call(functools.partial(collect_kernel, ctx, ch), in_specs=[pl.B...  25.8 us
    pallas_call x1, Pallas kernels, spread(): pl.pallas_call(functools.partial(spread_kernel, ctx, ch), in_specs=[hbm]...  21.2 us
    pallas_call x1, Pallas kernels, mix(): pl.pallas_call(mix_kernel, grid=(channels // block,), in_specs=[pl.BlockS...  9.52 us
    gather x1, local copies, waits for them, and re-layouts, shards(): jnp.take(gathered.reshape(ch * channels, taps), place, axis=0, mode='clip')  4.57 us
    gather x2, local copies, waits for them, and re-layouts, shards(): jnp.take(mirrored, place, axis=0, mode='clip').astype(F32)  3.07 us
    convert_element_type x1, other arithmetic, shards(): upstream = (cotangent.astype(F32) * query_input.astype(F32)).astype(BF16)  2.18 us
    reshape x1, local copies, waits for them, and re-layouts, shards(): mirrored = jnp.swapaxes(mirrored, 1, 2).reshape(ch * channels, share)  1.43 us

profile of v3, /device:TPU:0, one launch (start us, length us, event | category | flops | bytes accessed | tf_op | source)
XLA Modules:
  0.0 69.8 jit_solution(6748397588102125534)
XLA Ops:
  0.6 0.7 %fusion.3 = s32[1152]{0:T(1024)S(1)} fusion(s32[1152]{0:T(1024)} %param.19, s32[]{:T(128)S(6)} %axis_index.12), kind=kLoop, calls=%fused_computation.13 | loop fusion | flops 29952 | bytes 9220 | tf_op jit(solution)/shard_map/add | solution.py:293
  1.4 2.2 %multiply_convert_fusion = (bf16[128,1152]{1,0:T(8,128)(2,1)}, bf16[128,1152]{1,0:T(8,128)(2,1)}) fusion(bf16[128,1152]{1,0:T(8,128)(2,1)} %query.1, bf16[128,1152]{1,0:T(8,128)(2,1)} %cot.1, bf16[128,1152]{1,0:T(8,128)(2,1)} %value.1, bf16[128,1152]{1,0:T(8,128)(2,1)} %key.1), kind=kLoop, calls=%fused_computation.2 | loop fusion | flops 1179648 | bytes 1769472 | tf_op jit(solution)/shard_map/convert_element_type | solution.py:290
  3.6 21.2 %spread.1 = (bf16[128,1152]{1,0:T(8,128)(2,1)}, bf16[128,1152]{1,0:T(8,128)(2,1)}, bf16[128,1152]{1,0:T(8,128)(2,1)}, bf16[128,1152]{1,0:T(8,128)(2,1)}, bf16[4,1152,128]{2,1,0:T(8,128)(2,1)}) custom-call(bf16[128,1152]{1,0:T(8,128)(2,1)} %get-tuple-element.30.u, bf16[128,1152]{1,0:T(8,128)(2,1)} %get-tuple-element.29.r, bf16[1152,128]{1,0:T(8,128)(2,1)} %taps_own.1), custom_call_target="tpu_custom_call" | custom-call | tf_op jit(solution)/shard_map/spread/pallas_call | solution.py:220
  24.8 4.6 %gather_fusion = bf16[1152,128]{1,0:T(8,128)(2,1)} fusion(bf16[4608,128]{1,0:T(8,128)(2,1)} %bitcast.7, s32[2048]{0:T(1024)S(1)} %pad_clamp_fusion), kind=kCustom, calls=%fused_computation | custom fusion | bytes 594432 | tf_op jit(solution)/shard_map/jit(_take)/gather | solution.py:294
  29.4 9.5 %mix.1 = (bf16[128,1152]{1,0:T(8,128)(2,1)}, bf16[128,1152]{1,0:T(8,128)(2,1)}, bf16[128,1152]{1,0:T(8,128)(2,1)}, bf16[128,1152]{1,0:T(8,128)(2,1)}, bf16[256,1152]{1,0:T(8,128)(2,1)}) custom-call(s32[16]{0:T(128)} %lens.1, bf16[128,1152]{1,0:T(8,128)(2,1)} %query.1, bf16[128,1152]{1,0:T(8,128)(2,1)} %key.1, bf16[128,1152]{1,0:T(8,128)(2,1)} %value.1, ...), custom_call_target="tpu_custom_call" | custom-call | tf_op jit(solution)/shard_map/mix/pallas_call | solution.py:138
  38.9 25.8 %collect.1 = (f32[16,1152]{1,0:T(8,128)}, bf16[4,16,1152]{2,1,0:T(8,128)(2,1)}) custom-call(bf16[8,32,1152]{2,1,0:T(8,128)(2,1)} %bitcast.8), custom_call_target="tpu_custom_call" | custom-call | tf_op jit(solution)/shard_map/collect/pallas_call | solution.py:267
  64.7 1.4 %copy.24 = bf16[4,1152,16]{2,1,0:T(8,128)(2,1)S(1)} copy(bf16[4,1152,16]{1,2,0:T(8,128)(2,1)} %bitcast.9) | data formatting | bytes 294912 | tf_op jit(solution)/shard_map/reshape | solution.py:300
  66.1 0.0 copy-start
  66.1 2.9 %gather_fusion.1 = bf16[1152,16]{1,0:T(8,128)(2,1)S(1)} fusion(bf16[4608,16]{1,0:T(8,128)(2,1)S(1)} %bitcast.6, s32[2048]{0:T(1024)S(1)} %pad_clamp_fusion), kind=kCustom, calls=%fused_computation.1 | custom fusion | bytes 78336 | tf_op jit(solution)/shard_map/jit(_take)/gather | solution.py:301
  69.0 0.1 copy.23
  69.2 0.0 copy-done
  69.2 0.7 bitcast_add_fusion
  (1 shorter events, 0.0 us)
Async XLA Ops:
  66.1 3.1 %copy-start = (f32[16,1152]{1,0:T(8,128)S(1)}, f32[16,1152]{1,0:T(8,128)}, u32[]{:S(2)}) copy-start(f32[16,1152]{1,0:T(8,128)} %get-tuple-element.27) | copy-start | bytes 221188
